TPU v7x, 32 devices: a whole 2x2x4 slice. The times are simulated.
32 devices in a mesh: groups: 2 (over y), edge: 4 (over z), expert: 2 (over x), sys: 2 (over core).
Axes of the slice: x: 2, y: 2, z: 4, core: 2. Of those that a mesh axis runs over, the one named last changes fastest.
Arguments:
- edge_inputs: bfloat16 [8, 1792, 1280], P(('groups', 'expert', 'sys'), 'edge'), parts along dimension 0, may hold values from -6 to 6
- out_grad: bfloat16 [8, 1792, 1152], P(('groups', 'expert', 'sys'), 'edge'), parts along dimension 0, may hold values from -6 to 6
- expert_weights: bfloat16 [32, 1280, 1152], P('expert', 'edge'), may hold values from -0.15625 to 0.15625
- coef_table: float32 [16, 32], replicated, may hold values from 0.05 to 0.5
- system_kind: int32 [8], P('groups'), parts along dimension 0, may hold values from 0 to 15
- edge_counts: int32 [8], P('groups'), parts along dimension 0, may hold values from 896 to 1792, as said below
Outputs:
- input_grad: bfloat16 [8, 1792, 1280], P(('groups', 'expert', 'sys'), 'edge'), parts along dimension 0
- weight_grad: bfloat16 [64, 1280, 1152], P(('groups', 'expert'), 'edge'), parts along dimension 0
There are 2 independent parts, one for each index of `groups`. A program takes and returns all parts, laid end to end along the dimension named above; an argument that names none is the same for every part. Nothing has to cross between parts.
Inputs may be any that keep to these rules, and one draw needn't show every extreme that they name: `edge_counts`: the live edges of a system are its first ones. One system has all 1792 slots live and another exactly half of them.
All inputs are finite; a program needn't handle non-finite values.
Results may differ from a plain program's by a relative error of at most 0.018.
Values may be sent and summed in bfloat16 or wider, within the bound.
No kernel may reach another device: no remote copies, remote signals or barrier semaphores. Data moves between devices by JAX's collectives and lax.ppermute only.
A program may use at most 128 MiB of HBM per device.

v0:
```python
import functools
import math

import jax
import jax.numpy as jnp
from jax import lax
from jax.experimental import pallas as pl
from jax.experimental.pallas import tpu as pltpu
from jax.sharding import PartitionSpec as P


LAG, EVEN_LAG, ODD_LAG = 3, 3, 3
MERGED_AT = (6, 8)
SPREAD_BEFORE = (15, 20)
MIX_BEFORE = 8
ENDS_GRANT = 62 << 20


def entry(values, at):
    return values[min(at, len(values) - 1)] + 4 * max(0, at - len(values) + 1)


def plan(size, chunks):
    sums = {}
    rows = {}
    for h in range(chunks):
        for b in range(size):
            rows[b, b, h] = (entry(MERGED_AT, h), entry(MERGED_AT, h), None)
            if b > 0:
                sums[0, 1, b, h] = (0, 0, None)
            if b < size - 1:
                sums[size - 1, -1, b, h] = (0, 0, None)
    sent = set()
    steps = []
    total = 2 * chunks * size * (size - 1)
    while len(sent) < total:
        at = len(steps)
        step = []
        for low in range(at % 2, size - 1, 2):
            for source, way in ((low, 1), (low + 1, -1)):
                target = source + way
                left = size - 1 - target if way == 1 else target
                ready = []
                for h in range(chunks):
                    for b in range(size):
                        ahead = (b - target) * way
                        for kind, state, order in (
                            ("S", sums.get((source, way, b, h)) if ahead >= 0 else None, (-ahead - 2, 0, h)),
                            ("M", rows.get((source, b, h)) if (source - b) * way >= 0 else None, (-left, 1, h)),
                        ):
                            if state and state[0] <= at and (kind, source, way, b, h) not in sent:
                                ready.append(((state[1] > at, *order), (kind, b, h), state[2]))
                if ready:
                    _, (kind, b, h), came = min(ready, key=lambda choice: choice[0])
                    sent.add((kind, source, way, b, h))
                    step.append((source, target, kind, b, h, came))
        lag = ODD_LAG if at % 2 else EVEN_LAG
        for source, target, kind, b, h, _ in step:
            if kind == "M":
                rows[target, b, h] = (at + lag, at + LAG, at)
            elif b != target:
                sums[target, target - source, b, h] = (at + lag, at + LAG, at)
        steps.append(step)
    return steps


def at_device(values):
    place = lax.axis_index("edge")
    result = jnp.int32(values[0])
    for z in range(1, len(values)):
        if values[z] != values[z - 1]:
            result = jnp.where(place >= z, jnp.int32(values[z]), result)
    return result


def coefficient(table_ref, kind_ref, system, expert):
    return table_ref[kind_ref[system], expert]


def merge_kernel(expert_size, sys_size, first, tile, table_ref, kind_ref, weights_ref, *out_refs):
    experts, _, width = weights_ref.shape
    rows = out_refs[0].shape[0]
    place = lax.axis_index("expert")
    core = lax.axis_index("sys")
    factors = [
        [
            coefficient(table_ref, kind_ref, lax.rem(place + k, expert_size) * sys_size + core, place * experts + e)
            for e in range(experts)
        ]
        for k in range(expert_size)
    ]

    def step(block_ref, *parts):
        for start in range(0, tile, 16):
            span = pl.ds(start, 16)
            totals = [None] * expert_size
            for e in range(experts):
                weight = block_ref[e, span, :].astype(jnp.float32)
                for k in range(expert_size):
                    term = factors[k][e] * weight
                    totals[k] = term if totals[k] is None else totals[k] + term
            for k in range(expert_size):
                parts[k][span, :] = totals[k].astype(jnp.bfloat16)

    pltpu.emit_pipeline(
        step,
        grid=(rows // tile,),
        in_specs=[pl.BlockSpec((experts, tile, width), lambda i: (0, first // tile + i, 0))],
        out_specs=[pl.BlockSpec((tile, width), lambda i: (i, 0))] * expert_size,
    )(weights_ref, *out_refs)


def merge_part(table, kind, weights, expert_size, sys_size, first, rows, tile):
    experts, _, width = weights.shape
    return pl.pallas_call(
        functools.partial(merge_kernel, expert_size, sys_size, first, tile),
        in_specs=[
            pl.BlockSpec(memory_space=pltpu.SMEM),
            pl.BlockSpec(memory_space=pltpu.SMEM),
            pl.BlockSpec(memory_space=pltpu.HBM),
        ],
        out_specs=[pl.BlockSpec(memory_space=pl.ANY)] * expert_size,
        out_shape=[jax.ShapeDtypeStruct((rows, width), jnp.bfloat16)] * expert_size,
        compiler_params=pltpu.CompilerParams(vmem_limit_bytes=8 << 20),
        cost_estimate=pl.CostEstimate(
            flops=2 * expert_size * experts * rows * width,
            bytes_accessed=2 * experts * rows * width,
            transcendentals=0,
        ),
        name="merge",
    )(table, kind, weights)


def live_rows(grad_ref, counts_ref, sys_size):
    system = lax.axis_index("expert") * sys_size + lax.axis_index("sys")
    live = counts_ref[system] - lax.axis_index("edge") * grad_ref.shape[0]
    at = lax.broadcasted_iota(jnp.int32, grad_ref.shape, 0)
    return jnp.where(at < live, grad_ref[...], jnp.zeros((), grad_ref.dtype))


def ends_kernel(sys_size, rows, starts, span, counts_ref, features_ref, grad_ref, *refs):
    outs, (features, grad, product, ready) = refs[:-4], refs[-4:]
    lanes = features.shape[1]
    first = at_device(starts)
    window = pl.multiple_of(at_device([one // 128 * 128 if one + lanes <= span else span - lanes for one in starts]), 128)
    loads = [
        pltpu.make_async_copy(grad_ref, grad, ready.at[0]),
        pltpu.make_async_copy(features_ref.at[:, pl.ds(window, lanes)], features, ready.at[1]),
    ]
    for load in loads:
        load.start()
    for load in loads:
        load.wait()
    product[...] = lax.dot_general(
        features[...],
        live_rows(grad, counts_ref, sys_size),
        (((0,), (0,)), ((), ())),
        preferred_element_type=jnp.float32,
    ).astype(product.dtype)
    for h, out_ref in enumerate(outs):
        out_ref[...] = product[pl.ds(pl.multiple_of(first - window + h * rows, 16), rows), :]


def end_products(counts, features, grad, sys_size, edge_size, chunks, rows):
    edges, width_in = features.shape
    width = grad.shape[1]
    block = chunks * rows
    starts = [0 if z else (edge_size - 1) * block for z in range(edge_size)]
    lanes = max(-(-(one % 128 + block) // 128) * 128 for one in starts)
    return pl.pallas_call(
        functools.partial(ends_kernel, sys_size, rows, starts, width_in),
        in_specs=[
            pl.BlockSpec(memory_space=pltpu.SMEM),
            pl.BlockSpec(memory_space=pl.ANY),
            pl.BlockSpec(memory_space=pl.ANY),
        ],
        out_specs=[pl.BlockSpec(memory_space=pltpu.VMEM)] * chunks,
        out_shape=[jax.ShapeDtypeStruct((rows, width), jnp.bfloat16)] * chunks,
        scratch_shapes=[
            pltpu.VMEM((edges, lanes), jnp.bfloat16),
            pltpu.VMEM((edges, width), jnp.bfloat16),
            pltpu.VMEM((lanes, width), jnp.bfloat16),
            pltpu.SemaphoreType.DMA((2,)),
        ],
        compiler_params=pltpu.CompilerParams(vmem_limit_bytes=ENDS_GRANT),
        cost_estimate=pl.CostEstimate(
            flops=2 * edges * lanes * width, bytes_accessed=2 * edges * (lanes + width), transcendentals=0
        ),
        name="ends",
    )(counts, features, grad)


def outer_kernel(sys_size, counts_ref, features_ref, grad_ref, out_ref, masked):
    @pl.when(pl.program_id(0) == 0)
    def _():
        masked[...] = live_rows(grad_ref, counts_ref, sys_size)

    out_ref[...] = lax.dot_general(
        features_ref[...], masked[...], (((0,), (0,)), ((), ())), preferred_element_type=jnp.float32
    ).astype(out_ref.dtype)


def outer_products(counts, features, grad, sys_size, store_rows):
    edges, width_in = features.shape
    width = grad.shape[1]
    tile = 256 if width_in % 256 == 0 else width_in
    return pl.pallas_call(
        functools.partial(outer_kernel, sys_size),
        grid=(width_in // tile,),
        in_specs=[
            pl.BlockSpec(memory_space=pltpu.SMEM),
            pl.BlockSpec((edges, tile), lambda i: (0, i)),
            pl.BlockSpec((edges, width), lambda i: (0, 0)),
        ],
        out_specs=pl.BlockSpec((tile, width), lambda i: (i, 0)),
        out_shape=jax.ShapeDtypeStruct((store_rows, width), jnp.bfloat16),
        scratch_shapes=[pltpu.VMEM((edges, width), jnp.bfloat16)],
        compiler_params=pltpu.CompilerParams(vmem_limit_bytes=12 << 20),
        cost_estimate=pl.CostEstimate(
            flops=2 * edges * width_in * width,
            bytes_accessed=2 * (edges * width_in + edges * width + width_in * width),
            transcendentals=0,
        ),
        name="outer",
    )(counts, features, grad)


def input_kernel(sys_size, counts_ref, grad_ref, rows_ref, out_ref, live_ref):
    @pl.when(pl.program_id(0) == 0)
    def _():
        live_ref[...] = live_rows(grad_ref, counts_ref, sys_size)

    out_ref[...] = lax.dot_general(
        live_ref[...], rows_ref[...], (((1,), (1,)), ((), ())), preferred_element_type=jnp.float32
    ).astype(out_ref.dtype)


def input_product(counts, grad, store, sys_size, width_in):
    edges, width = grad.shape
    tile = 256 if width_in % 256 == 0 else width_in
    return pl.pallas_call(
        functools.partial(input_kernel, sys_size),
        grid=(width_in // tile,),
        in_specs=[
            pl.BlockSpec(memory_space=pltpu.SMEM),
            pl.BlockSpec((edges, width), lambda i: (0, 0)),
            pl.BlockSpec((tile, width), lambda i: (width_in // tile + i, 0)),
        ],
        out_specs=[
            pl.BlockSpec((edges, tile), lambda i: (0, i)),
            pl.BlockSpec((edges, width), lambda i: (0, 0)),
        ],
        out_shape=[
            jax.ShapeDtypeStruct((edges, width_in), jnp.bfloat16),
            jax.ShapeDtypeStruct((edges, width), jnp.bfloat16),
        ],
        compiler_params=pltpu.CompilerParams(vmem_limit_bytes=12 << 20),
        cost_estimate=pl.CostEstimate(
            flops=2 * edges * width_in * width,
            bytes_accessed=2 * (edges * width_in + edges * width + width_in * width),
            transcendentals=0,
        ),
        name="input_product",
    )(counts, grad, store)


def last_kernel(width_in, windows, live_ref, store_ref, _, out_ref, part, done):
    lanes = part.shape[1]
    first = pl.multiple_of(at_device(windows), 128)
    part[...] = lax.dot_general(
        live_ref[...],
        store_ref[pl.ds(pl.multiple_of(width_in + first, 128), lanes), :],
        (((1,), (1,)), ((), ())),
        preferred_element_type=jnp.float32,
    ).astype(part.dtype)
    write = pltpu.make_async_copy(part, out_ref.at[:, pl.ds(first, lanes)], done)
    write.start()
    write.wait()


def last_product(live, store, product, rows, places):
    edges, width_in = product.shape
    lanes = min(width_in, max(-(-(place * rows % 128 + rows) // 128) * 128 for place in places))
    windows = [min(place * rows // 128 * 128, width_in - lanes) for place in places]
    vmem = pl.BlockSpec(memory_space=pltpu.VMEM)
    return pl.pallas_call(
        functools.partial(last_kernel, width_in, windows),
        in_specs=[vmem, vmem, pl.BlockSpec(memory_space=pl.ANY)],
        out_specs=pl.BlockSpec(memory_space=pl.ANY),
        out_shape=jax.ShapeDtypeStruct(product.shape, product.dtype),
        input_output_aliases={2: 0},
        scratch_shapes=[pltpu.VMEM((edges, lanes), jnp.bfloat16), pltpu.SemaphoreType.DMA],
        compiler_params=pltpu.CompilerParams(vmem_limit_bytes=4 << 20),
        cost_estimate=pl.CostEstimate(
            flops=2 * edges * lanes * live.shape[1], bytes_accessed=2 * edges * lanes, transcendentals=0
        ),
        name="last_product",
    )(live, store, product)


def hop_kernel(count, behind, take, add, send, rows, *refs):
    arrays, (store, *message) = refs[1 : 1 + count], refs[1 + count + behind :]
    if count:
        into = at_device(take) * rows
        adds = at_device(add) == 1
    if send is not None:
        origin = at_device(send) * rows

    if count:

        def update(i, _):
            span = pl.ds(pl.multiple_of(i * 16, 16), 16)
            here = pl.ds(pl.multiple_of(into + i * 16, 16), 16)
            total = arrays[0][span, :].astype(jnp.float32)
            for ref in arrays[1:]:
                total = total + ref[span, :].astype(jnp.float32)
            total = jnp.where(adds, store[here, :].astype(jnp.float32) + total, total)
            store[here, :] = total.astype(store.dtype)
            return 0

        lax.fori_loop(0, rows // 16, update, 0)
    if send is not None:

        def copy(i, _):
            span = pl.ds(pl.multiple_of(i * 16, 16), 16)
            message[0][span, :] = store[pl.ds(pl.multiple_of(origin + i * 16, 16), 16), :]
            return 0

        lax.fori_loop(0, rows // 16, copy, 0)


def hop(store, arrays, take, add, send, rows, behind=()):
    width = store.shape[1]
    vmem = pl.BlockSpec(memory_space=pltpu.VMEM)
    shapes = [jax.ShapeDtypeStruct(store.shape, store.dtype)]
    if send is not None:
        shapes.append(jax.ShapeDtypeStruct((rows, width), store.dtype))
    return pl.pallas_call(
        functools.partial(hop_kernel, len(arrays), len(behind), take, add, send, rows),
        in_specs=[vmem] * (1 + len(arrays)) + [pl.BlockSpec(memory_space=pl.ANY)] * len(behind),
        out_specs=[vmem] * len(shapes),
        out_shape=shapes,
        input_output_aliases={0: 0},
        compiler_params=pltpu.CompilerParams(vmem_limit_bytes=1 << 20),
        cost_estimate=pl.CostEstimate(flops=rows * width, bytes_accessed=4 * rows * width, transcendentals=0),
        name="hop",
    )(store, *arrays, *behind)


def mix_kernel(expert_size, sys_size, scale, tile, table_ref, kind_ref, out_ref):
    width = out_ref.shape[1]
    slots = expert_size * sys_size
    experts = out_ref.shape[0] // tile
    place = lax.axis_index("expert")
    core = lax.axis_index("sys")
    line = lax.broadcasted_iota(jnp.int32, (tile, width), 0)
    lane = lax.broadcasted_iota(jnp.int32, (tile, width), 1)
    upper = lane < slots * tile
    lane = jnp.where(upper, lane, lane - slots * tile)
    slot_at = lane // tile
    hit = (lane - slot_at * tile) == line
    systems = [
        lax.rem(place + expert_size - k, expert_size) * sys_size + lax.rem(core + sys_size - l, sys_size)
        for l in range(sys_size)
        for k in range(expert_size)
    ]
    for e in range(experts):
        value = jnp.zeros((tile, width), jnp.float32)
        for slot, system in enumerate(systems):
            factor = coefficient(table_ref, kind_ref, system, place * experts + e) * scale
            value = jnp.where(slot_at == slot, factor, value)
        high = value.astype(jnp.bfloat16)
        low = (value - high.astype(jnp.float32)).astype(jnp.bfloat16)
        value = jnp.where(upper, high.astype(jnp.float32), low.astype(jnp.float32))
        out_ref[pl.ds(e * tile, tile), :] = jnp.where(hit, value, 0.0).astype(jnp.bfloat16)


def mix_matrix(table, kind, expert_size, sys_size, experts, scale, tile):
    width = 2 * expert_size * sys_size * tile
    return pl.pallas_call(
        functools.partial(mix_kernel, expert_size, sys_size, scale, tile),
        in_specs=[pl.BlockSpec(memory_space=pltpu.SMEM)] * 2,
        out_specs=pl.BlockSpec(memory_space=pltpu.VMEM),
        out_shape=jax.ShapeDtypeStruct((experts * tile, width), jnp.bfloat16),
        compiler_params=pltpu.CompilerParams(vmem_limit_bytes=4 << 20),
        cost_estimate=pl.CostEstimate(flops=10 * experts * tile * width, bytes_accessed=0, transcendentals=0),
        name="mix",
    )(table, kind)


def spread_kernel(count, groups, mix_ref, *refs):
    out_ref, token_ref = refs[-2:]
    token_ref[...] = jnp.zeros_like(token_ref)
    experts, tile, width = out_ref.shape
    rows = jnp.concatenate([ref[...] for ref in refs[:count]], axis=0)
    rows = jnp.concatenate([rows, rows], axis=0)
    span = experts // groups
    for g in range(groups):
        part = jnp.dot(
            mix_ref[pl.ds(g * span * tile, span * tile), :], rows, preferred_element_type=jnp.float32
        )
        out_ref[pl.ds(g * span, span)] = part.astype(out_ref.dtype).reshape(span, tile, width)


def spread(mix, pieces, previous, experts, first, rows_all, tile):
    rows, width = pieces[0].shape
    count = len(pieces)
    groups = 4 if experts % 4 == 0 else 1
    specs = [pl.BlockSpec(mix.shape, lambda i: (0, 0))]
    specs += [pl.BlockSpec((tile, width), lambda i: (i, 0))] * count
    operands = [mix, *pieces]
    aliases = {}
    if previous is not None:
        specs.append(pl.BlockSpec(memory_space=pl.ANY))
        operands.append(previous)
        aliases = {len(operands) - 1: 0}
    return pl.pallas_call(
        functools.partial(spread_kernel, count, groups),
        grid=(rows // tile,),
        in_specs=specs,
        out_specs=[
            pl.BlockSpec((experts, tile, width), lambda i: (0, first // tile + i, 0)),
            pl.BlockSpec((8, 128), lambda i: (0, 0)),
        ],
        out_shape=[
            jax.ShapeDtypeStruct((experts, rows_all, width), jnp.bfloat16),
            jax.ShapeDtypeStruct((8, 128), jnp.float32),
        ],
        input_output_aliases=aliases,
        compiler_params=pltpu.CompilerParams(vmem_limit_bytes=16 << 20),
        cost_estimate=pl.CostEstimate(
            flops=2 * mix.size * rows // tile * width, bytes_accessed=2 * experts * rows * width, transcendentals=0
        ),
        name="spread",
    )(*operands)


def swaps(at, edge_size, sys_size):
    pairs = []
    for z in range(edge_size):
        other = z + 1 if (z - at) % 2 == 0 else z - 1
        for core in range(sys_size):
            if 0 <= other < edge_size:
                pairs.append((z * sys_size + core, other * sys_size + core))
            elif sys_size % 2 == 0:
                pairs.append((z * sys_size + core, z * sys_size + (core ^ 1)))
    return pairs


def shift(size, by):
    return [(i, (i + by) % size) for i in range(size)]


def chunks_of(row_count):
    return 2 if row_count % 32 == 0 else 1


def body(edge_inputs, out_grad, expert_weights, coef_table, system_kind, edge_counts):
    edge_size = lax.axis_size("edge")
    expert_size = lax.axis_size("expert")
    sys_size = lax.axis_size("sys")
    exp_local, row_count, _ = expert_weights.shape
    width_in = edge_inputs.shape[2]
    edge_rows = out_grad.shape[1]
    chunks = chunks_of(row_count)
    rows = row_count // chunks
    tile = 32 if rows % 32 == 0 else 16
    features, grad = edge_inputs[0], out_grad[0]
    places = edge_size * chunks
    spare = 2 * places

    scale = 1.0 / math.sqrt(edge_rows * edge_size)
    mix = mix_matrix(coef_table, system_kind, expert_size, sys_size, exp_local, scale, tile)

    firsts = end_products(edge_counts, features, grad, sys_size, edge_size, chunks, rows)
    store = outer_products(edge_counts, features, grad, sys_size, (2 * places + 1) * rows)
    exchanged = []
    for h in range(chunks):
        parts = merge_part(
            coef_table, system_kind, expert_weights, expert_size, sys_size, h * rows, rows, tile
        )
        arrays = [parts[0]]
        arrays += [lax.ppermute(parts[k], "expert", shift(expert_size, k)) for k in range(1, expert_size)]
        exchanged.append(arrays)

    steps = plan(edge_size, chunks)
    pending = []
    got = {}
    merged = set()
    waiting = {h: 2 * edge_size - 2 for h in range(chunks)}
    taken = set()
    result = None

    def own(first):
        return [first + z * chunks for z in range(edge_size)]

    def settle(store, at, origin, behind=()):
        take, add = [spare] * edge_size, [0] * edge_size
        for _, target, kind, b, h, _ in steps[at]:
            take[target] = b * chunks + h + (places if kind == "M" else 0)
            add[target] = int(kind == "S")
            if kind == "S" and b == target:
                waiting[h] -= 1
        pending.remove(at)
        return hop(store, [got.pop(at)], take, add, origin, rows, behind)

    tokens = {}
    mixed = [mix]

    def overdue(at):
        late = [tokens.pop(h) for h in list(tokens) if at >= entry(SPREAD_BEFORE, h)]
        if mixed and at >= MIX_BEFORE:
            late.append(mixed.pop())
        return late

    def finish(store, result):
        for h in range(chunks):
            if waiting[h] or h in taken:
                continue
            taken.add(h)
            store, rows_h = hop(store, [], None, None, own(h), rows)
            column = [rows_h]
            for k in range(1, expert_size):
                column.append(lax.ppermute(rows_h, "expert", shift(expert_size, k)))
            pieces = list(column)
            for l in range(1, sys_size):
                pieces += [lax.ppermute(piece, "sys", shift(sys_size, l)) for piece in column]
            result, token = spread(mix, pieces, result, exp_local, h * rows, row_count, tile)
            tokens[h] = token
        return store, result

    for at, step in enumerate(steps):
        if not step:
            continue
        for source, _, kind, b, h, _ in step:
            if kind == "M" and b == source and h not in merged:
                merged.add(h)
                (store,) = hop(store, exchanged[h], own(places + h), [0] * edge_size, None, rows)
        origin = [spare] * edge_size
        for source, _, kind, b, h, _ in step:
            origin[source] = b * chunks + h + (places if kind == "M" else 0)
        needed = {came for *_, came in step}
        due = [one for one in pending if one in needed or one <= at - LAG]
        for one in due[:-1]:
            (store,) = settle(store, one, None)
        if all((kind, b) == ("S", 0 if source else edge_size - 1) and came is None for source, _, kind, b, _, came in step):
            message = firsts[step[0][4]]
        elif due:
            store, message = settle(store, due[-1], origin, overdue(at))
        else:
            store, message = hop(store, [], None, None, origin, rows, overdue(at))
        got[at] = lax.ppermute(message, ("edge", "sys"), swaps(at, edge_size, sys_size))
        pending.append(at)
        store, result = finish(store, result)
    while len(pending) > 1:
        (store,) = settle(store, pending[0], None, list(tokens.values()) if len(pending) == 2 else ())
        store, result = finish(store, result)
    product, live = input_product(edge_counts, grad, store, sys_size, width_in)
    last = [0] * edge_size
    for _, target, _, b, h, _ in steps[pending[0]]:
        last[target] = b * chunks + h
    (store,) = settle(store, pending[0], None, (live,))
    store, result = finish(store, result)
    input_grad = last_product(live, store, product, rows, last)
    return (input_grad[None], result)


def solution(mesh):
    specs = dict(
        mesh=mesh,
        in_specs=(
            P(("groups", "expert", "sys"), "edge", None),
            P(("groups", "expert", "sys"), "edge", None),
            P("expert", "edge", None),
            P(),
            P("groups"),
            P("groups"),
        ),
        out_specs=(
            P(("groups", "expert", "sys"), "edge", None),
            P(("groups", "expert"), "edge", None),
        ),
        check_vma=False,
    )

    def program(*args):
        return jax.shard_map(body, **specs)(*args)

    return program
```

profile of v0, /device:TPU:0, one launch (start us, length us, event | category | flops | bytes accessed | tf_op | source)
XLA Modules:
  0.0 107.4 jit_solution(7442383361138122486)
XLA Ops:
  0.6 3.6 %ends.1 = (bf16[160,1152]{1,0:T(8,128)(2,1)}, bf16[160,1152]{1,0:T(8,128)(2,1)}) custom-call(s32[4]{0:T(128)} %counts_ref.5, bf16[448,1280]{1,0:T(8,128)(2,1)} %bitcast.8, bf16[448,1152]{1,0:T(8,128)(2,1)} %bitcast.5), custom_call_target="tpu_custom_call" | custom-call | flops 396361728 | bytes 1376256 | tf_op jit(solution)/shard_map/ends/pallas_call | solution.py:170
  4.3 3.1 %collective-permute-start = (bf16[160,1152]{1,0:T(8,128)(2,1)}, bf16[160,1152]{1,0:T(8,128)(2,1)S(1)}, u32[]{:S(2)}, u32[]{:S(2)}) collective-permute-start(bf16[160,1152]{1,0:T(8,128)(2,1)} %get-tuple-element.52), channel_id=1, source_target_pairs={{0,4},{1,5},{4,0},{5,1},{8,12},{9,13},{12,8},{13,9},{2,6},{3,7},{6... | collective-permute-start | bytes 1105928 | tf_op jit(solution)/shard_map/ppermute | solution.py:552
  10.6 3.8 %outer.1.refs_0_ = bf16[2720,1152]{1,0:T(8,128)(2,1)S(1)} custom-call(s32[4]{0:T(128)S(1)} %copy-done.5, bf16[448,1280]{1,0:T(8,128)(2,1)S(1)} %bitcast.9, bf16[448,1152]{1,0:T(8,128)(2,1)S(1)} %bitcast.6), custom_call_target="tpu_custom_call" | custom-call | flops 1321205760 | bytes 5128192 | tf_op jit(solution)/shard_map/outer/pallas_call | solution.py:207
  14.4 2.6 %collective-permute-done.refs_1_ = bf16[160,1152]{1,0:T(8,128)(2,1)S(1)} collective-permute-done((bf16[160,1152]{1,0:T(8,128)(2,1)}, bf16[160,1152]{1,0:T(8,128)(2,1)S(1)}, u32[]{:S(2)}, u32[]{:S(2)}) %collective-permute-start) | collective-permute-done | bytes 368672 | tf_op jit(solution)/shard_map/ppermute | solution.py:552
  17.5 3.6 %collective-permute-start.3 = (bf16[160,1152]{1,0:T(8,128)(2,1)S(1)}, bf16[160,1152]{1,0:T(8,128)(2,1)S(1)}, u32[]{:S(2)}, u32[]{:S(2)}) collective-permute-start(bf16[160,1152]{1,0:T(8,128)(2,1)S(1)} %get-tuple-element.59), channel_id=1, source_target_pairs={{0,4},{1,5},{4,0},{5,1},{8,12},{9,13},{12,8},{13,9},{2,6},{3,7},{6... | collective-permute-start | bytes 1105928 | tf_op jit(solution)/shard_map/ppermute | solution.py:552
  21.1 3.9 %collective-permute-done.1.refs_1_ = bf16[160,1152]{1,0:T(8,128)(2,1)S(1)} collective-permute-done((bf16[160,1152]{1,0:T(8,128)(2,1)}, bf16[160,1152]{1,0:T(8,128)(2,1)S(1)}, u32[]{:S(2)}, u32[]{:S(2)}) %collective-permute-start.1) | collective-permute-done | bytes 368672 | tf_op jit(solution)/shard_map/ppermute | solution.py:552
  25.3 4.4 %merge.2 = (bf16[160,1152]{1,0:T(8,128)(2,1)S(1)}, bf16[160,1152]{1,0:T(8,128)(2,1)S(1)}) custom-call(f32[16,32]{1,0:T(8,128)S(1)} %copy-done.3, s32[4]{0:T(128)S(1)} %copy-done.4, bf16[16,320,1152]{2,1,0:T(8,128)(2,1)S(1)} %bitcast.4), custom_call_target="tpu_custom_call" | custom-call | flops 11796480 | bytes 5898240 | tf_op jit(solution)/shard_map/merge/pallas_call | solution.py:115
  29.7 2.0 %collective-permute-start.6 = (bf16[160,1152]{1,0:T(8,128)(2,1)S(1)}, bf16[160,1152]{1,0:T(8,128)(2,1)S(1)}, u32[]{:S(2)}, u32[]{:S(2)}) collective-permute-start(bf16[160,1152]{1,0:T(8,128)(2,1)S(1)} %get-tuple-element.66), channel_id=1, source_target_pairs={{0,2},{2,0},{1,3},{3,1},{4,6},{6,4},{5,7},{7,5},{8,10},{10,8},{9,1... | collective-permute-start | bytes 1105928 | tf_op jit(solution)/shard_map/ppermute | solution.py:483
  32.8 3.2 %collective-permute-start.5 = (bf16[160,1152]{1,0:T(8,128)(2,1)S(1)}, bf16[160,1152]{1,0:T(8,128)(2,1)S(1)}, u32[]{:S(2)}, u32[]{:S(2)}) collective-permute-start(bf16[160,1152]{1,0:T(8,128)(2,1)S(1)} %get-tuple-element.63), channel_id=1, source_target_pairs={{0,4},{1,5},{4,0},{5,1},{8,12},{9,13},{12,8},{13,9},{2,6},{3,7},{6... | collective-permute-start | bytes 1105928 | tf_op jit(solution)/shard_map/ppermute | solution.py:552
  38.2 4.4 %merge.3 = (bf16[160,1152]{1,0:T(8,128)(2,1)S(1)}, bf16[160,1152]{1,0:T(8,128)(2,1)S(1)}) custom-call(f32[16,32]{1,0:T(8,128)S(1)} %copy-done.3, s32[4]{0:T(128)S(1)} %copy-done.4, bf16[16,320,1152]{2,1,0:T(8,128)(2,1)S(1)} %bitcast.4), custom_call_target="tpu_custom_call" | custom-call | flops 11796480 | bytes 5898240 | tf_op jit(solution)/shard_map/merge/pallas_call | solution.py:115
  43.1 2.2 %collective-permute-done.5.refs_1_ = bf16[160,1152]{1,0:T(8,128)(2,1)S(1)} collective-permute-done((bf16[160,1152]{1,0:T(8,128)(2,1)S(1)}, bf16[160,1152]{1,0:T(8,128)(2,1)S(1)}, u32[]{:S(2)}, u32[]{:S(2)}) %collective-permute-start.5) | collective-permute-done | bytes 368672 | tf_op jit(solution)/shard_map/ppermute | solution.py:552
  46.0 5.4 %collective-permute-done.8.refs_1_ = bf16[160,1152]{1,0:T(8,128)(2,1)S(1)} collective-permute-done((bf16[160,1152]{1,0:T(8,128)(2,1)S(1)}, bf16[160,1152]{1,0:T(8,128)(2,1)S(1)}, u32[]{:S(2)}, u32[]{:S(2)}) %collective-permute-start.8) | collective-permute-done | bytes 368672 | tf_op jit(solution)/shard_map/ppermute | solution.py:552
  52.1 3.2 %collective-permute-start.11 = (bf16[160,1152]{1,0:T(8,128)(2,1)S(1)}, bf16[160,1152]{1,0:T(8,128)(2,1)S(1)}, u32[]{:S(2)}, u32[]{:S(2)}) collective-permute-start(bf16[160,1152]{1,0:T(8,128)(2,1)S(1)} %get-tuple-element.76), channel_id=1, source_target_pairs={{0,4},{1,5},{4,0},{5,1},{8,12},{9,13},{12,8},{13,9},{2,6},{3,7},{6... | collective-permute-start | bytes 1105928 | tf_op jit(solution)/shard_map/ppermute | solution.py:552
  55.8 4.7 %collective-permute-done.14.refs_1_ = bf16[160,1152]{1,0:T(8,128)(2,1)S(1)} collective-permute-done((bf16[160,1152]{1,0:T(8,128)(2,1)S(1)}, bf16[160,1152]{1,0:T(8,128)(2,1)S(1)}, u32[]{:S(2)}, u32[]{:S(2)}) %collective-permute-start.14) | collective-permute-done | bytes 368672 | tf_op jit(solution)/shard_map/ppermute | solution.py:524
  61.0 4.1 %collective-permute-start.13 = (bf16[160,1152]{1,0:T(8,128)(2,1)S(1)}, bf16[160,1152]{1,0:T(8,128)(2,1)S(1)}, u32[]{:S(2)}, u32[]{:S(2)}) collective-permute-start(bf16[160,1152]{1,0:T(8,128)(2,1)S(1)} %get-tuple-element.81), channel_id=1, source_target_pairs={{0,4},{1,5},{4,0},{5,1},{8,12},{9,13},{12,8},{13,9},{2,6},{3,7},{6... | collective-permute-start | bytes 1105928 | tf_op jit(solution)/shard_map/ppermute | solution.py:552
  67.1 7.2 %collective-permute-start.18 = (bf16[160,1152]{1,0:T(8,128)(2,1)S(1)}, bf16[160,1152]{1,0:T(8,128)(2,1)S(1)}, u32[]{:S(2)}, u32[]{:S(2)}) collective-permute-start(bf16[160,1152]{1,0:T(8,128)(2,1)S(1)} %get-tuple-element.87), channel_id=1, source_target_pairs={{0,4},{1,5},{4,0},{5,1},{8,12},{9,13},{12,8},{13,9},{2,6},{3,7},{6... | collective-permute-start | bytes 1105928 | tf_op jit(solution)/shard_map/ppermute | solution.py:552
  74.3 4.6 %spread.2 = (bf16[16,320,1152]{2,1,0:T(8,128)(2,1)}, f32[8,128]{1,0:T(8,128)S(1)}) custom-call(bf16[512,256]{1,0:T(8,128)(2,1)S(1)} %mix.1.refs_2_.mix_ref, bf16[160,1152]{1,0:T(8,128)(2,1)S(1)} %get-tuple-element.82.refs_0_, bf16[160,1152]{1,0:T(8,128)(2,1)S(1)} %collective-permute-done.14.refs_1_, bf16[160,1152]{1,0:T(8,128)(2,1)S(1)} %collective-permute-done.15.refs_2_, ...), custom_call_target="tpu_custom_call" | custom-call | flops 1509949440 | bytes 5898240 | tf_op jit(solution)/shard_map/spread/pallas_call | solution.py:417
  79.3 2.1 %collective-permute-start.20 = (bf16[160,1152]{1,0:T(8,128)(2,1)S(1)}, bf16[160,1152]{1,0:T(8,128)(2,1)S(1)}, u32[]{:S(2)}, u32[]{:S(2)}) collective-permute-start(bf16[160,1152]{1,0:T(8,128)(2,1)S(1)} %get-tuple-element.91), channel_id=1, source_target_pairs={{0,4},{1,5},{4,0},{5,1},{8,12},{9,13},{12,8},{13,9},{2,6},{3,7},{6... | collective-permute-start | bytes 1105928 | tf_op jit(solution)/shard_map/ppermute | solution.py:552
  82.3 6.1 %collective-permute-start.25 = (bf16[160,1152]{1,0:T(8,128)(2,1)S(1)}, bf16[160,1152]{1,0:T(8,128)(2,1)S(1)}, u32[]{:S(2)}, u32[]{:S(2)}) collective-permute-start(bf16[160,1152]{1,0:T(8,128)(2,1)S(1)} %get-tuple-element.97), channel_id=1, source_target_pairs={{0,4},{1,5},{4,0},{5,1},{8,12},{9,13},{12,8},{13,9},{2,6},{3,7},{6... | collective-permute-start | bytes 1105928 | tf_op jit(solution)/shard_map/ppermute | solution.py:552
  88.4 2.4 %collective-permute-done.20.refs_1_ = bf16[160,1152]{1,0:T(8,128)(2,1)S(1)} collective-permute-done((bf16[160,1152]{1,0:T(8,128)(2,1)S(1)}, bf16[160,1152]{1,0:T(8,128)(2,1)S(1)}, u32[]{:S(2)}, u32[]{:S(2)}) %collective-permute-start.20) | collective-permute-done | bytes 368672 | tf_op jit(solution)/shard_map/ppermute | solution.py:552
  90.9 4.6 %spread.3 = (bf16[16,320,1152]{2,1,0:T(8,128)(2,1)}, f32[8,128]{1,0:T(8,128)S(1)}) custom-call(bf16[512,256]{1,0:T(8,128)(2,1)S(1)} %mix.1.refs_2_.mix_ref, bf16[160,1152]{1,0:T(8,128)(2,1)S(1)} %get-tuple-element.93.refs_0_, bf16[160,1152]{1,0:T(8,128)(2,1)S(1)} %collective-permute-done.22.refs_1_, ...), custom_call_target="tpu_custom_call", output_to_operand_aliasing={{0}: (5, {})} | custom-call | flops 1509949440 | bytes 5898240 | tf_op jit(solution)/shard_map/spread/pallas_call | solution.py:417
  95.7 2.1 %collective-permute-start.26 = (bf16[160,1152]{1,0:T(8,128)(2,1)S(1)}, bf16[160,1152]{1,0:T(8,128)(2,1)S(1)}, u32[]{:S(2)}, u32[]{:S(2)}) collective-permute-start(bf16[160,1152]{1,0:T(8,128)(2,1)S(1)} %get-tuple-element.99), channel_id=1, source_target_pairs={{0,4},{1,5},{4,0},{5,1},{8,12},{9,13},{12,8},{13,9},{2,6},{3,7},{6... | collective-permute-start | bytes 1105928 | tf_op jit(solution)/shard_map/ppermute | solution.py:552
  99.9 4.2 %input_product.1 = (bf16[448,1280]{1,0:T(8,128)(2,1)}, bf16[448,1152]{1,0:T(8,128)(2,1)S(1)}) custom-call(s32[4]{0:T(128)S(1)} %copy-done.6, bf16[448,1152]{1,0:T(8,128)(2,1)S(1)} %bitcast.7, bf16[2720,1152]{1,0:T(8,128)(2,1)S(1)} %hop.46.rows_ref.refs_0_), custom_call_target="tpu_custom_call" | custom-call | flops 1321205760 | bytes 5128192 | tf_op jit(solution)/shard_map/input_product/pallas_call | solution.py:241
  104.2 1.9 %collective-permute-done.26.refs_1_ = bf16[160,1152]{1,0:T(8,128)(2,1)S(1)} collective-permute-done((bf16[160,1152]{1,0:T(8,128)(2,1)S(1)}, bf16[160,1152]{1,0:T(8,128)(2,1)S(1)}, u32[]{:S(2)}, u32[]{:S(2)}) %collective-permute-start.26) | collective-permute-done | bytes 368672 | tf_op jit(solution)/shard_map/ppermute | solution.py:552
  (84 shorter events, 16.9 us)
Async XLA Ops:
  4.3 12.7 %collective-permute-start = (bf16[160,1152]{1,0:T(8,128)(2,1)}, bf16[160,1152]{1,0:T(8,128)(2,1)S(1)}, u32[]{:S(2)}, u32[]{:S(2)}) collective-permute-start(bf16[160,1152]{1,0:T(8,128)(2,1)} %get-tuple-element.52), channel_id=1, source_target_pairs={{0,4},{1,5},{4,0},{5,1},{8,12},{9,13},{12,8},{13,9},{2,6},{3,7},{6... | collective-permute-start | bytes 1105928 | tf_op jit(solution)/shard_map/ppermute | solution.py:552
  7.4 17.5 %collective-permute-start.1 = (bf16[160,1152]{1,0:T(8,128)(2,1)}, bf16[160,1152]{1,0:T(8,128)(2,1)S(1)}, u32[]{:S(2)}, u32[]{:S(2)}) collective-permute-start(bf16[160,1152]{1,0:T(8,128)(2,1)} %get-tuple-element.55), channel_id=1, source_target_pairs={{0,4},{1,5},{4,0},{5,1},{8,12},{9,13},{12,8},{13,9},{2,6},{3,7},{6... | collective-permute-start | bytes 1105928 | tf_op jit(solution)/shard_map/ppermute | solution.py:552
  17.3 15.2 %collective-permute-start.2 = (bf16[160,1152]{1,0:T(8,128)(2,1)S(1)}, bf16[160,1152]{1,0:T(8,128)(2,1)S(1)}, u32[]{:S(2)}, u32[]{:S(2)}) collective-permute-start(bf16[160,1152]{1,0:T(8,128)(2,1)S(1)} %get-tuple-element.57), channel_id=1, source_target_pairs={{0,1},{1,0},{4,8},{5,9},{8,4},{9,5},{12,13},{13,12},{2,3},{3,2},{6... | collective-permute-start | bytes 1105928 | tf_op jit(solution)/shard_map/ppermute | solution.py:552
  17.5 18.5 %collective-permute-start.3 = (bf16[160,1152]{1,0:T(8,128)(2,1)S(1)}, bf16[160,1152]{1,0:T(8,128)(2,1)S(1)}, u32[]{:S(2)}, u32[]{:S(2)}) collective-permute-start(bf16[160,1152]{1,0:T(8,128)(2,1)S(1)} %get-tuple-element.59), channel_id=1, source_target_pairs={{0,4},{1,5},{4,0},{5,1},{8,12},{9,13},{12,8},{13,9},{2,6},{3,7},{6... | collective-permute-start | bytes 1105928 | tf_op jit(solution)/shard_map/ppermute | solution.py:552
  25.2 11.1 %collective-permute-start.4 = (bf16[160,1152]{1,0:T(8,128)(2,1)S(1)}, bf16[160,1152]{1,0:T(8,128)(2,1)S(1)}, u32[]{:S(2)}, u32[]{:S(2)}) collective-permute-start(bf16[160,1152]{1,0:T(8,128)(2,1)S(1)} %get-tuple-element.61), channel_id=1, source_target_pairs={{0,1},{1,0},{4,8},{5,9},{8,4},{9,5},{12,13},{13,12},{2,3},{3,2},{6... | collective-permute-start | bytes 1105928 | tf_op jit(solution)/shard_map/ppermute | solution.py:552
  29.7 15.9 %collective-permute-start.6 = (bf16[160,1152]{1,0:T(8,128)(2,1)S(1)}, bf16[160,1152]{1,0:T(8,128)(2,1)S(1)}, u32[]{:S(2)}, u32[]{:S(2)}) collective-permute-start(bf16[160,1152]{1,0:T(8,128)(2,1)S(1)} %get-tuple-element.66), channel_id=1, source_target_pairs={{0,2},{2,0},{1,3},{3,1},{4,6},{6,4},{5,7},{7,5},{8,10},{10,8},{9,1... | collective-permute-start | bytes 1105928 | tf_op jit(solution)/shard_map/ppermute | solution.py:483
  32.8 12.6 %collective-permute-start.5 = (bf16[160,1152]{1,0:T(8,128)(2,1)S(1)}, bf16[160,1152]{1,0:T(8,128)(2,1)S(1)}, u32[]{:S(2)}, u32[]{:S(2)}) collective-permute-start(bf16[160,1152]{1,0:T(8,128)(2,1)S(1)} %get-tuple-element.63), channel_id=1, source_target_pairs={{0,4},{1,5},{4,0},{5,1},{8,12},{9,13},{12,8},{13,9},{2,6},{3,7},{6... | collective-permute-start | bytes 1105928 | tf_op jit(solution)/shard_map/ppermute | solution.py:552
  36.2 9.6 %collective-permute-start.7 = (bf16[160,1152]{1,0:T(8,128)(2,1)S(1)}, bf16[160,1152]{1,0:T(8,128)(2,1)S(1)}, u32[]{:S(2)}, u32[]{:S(2)}) collective-permute-start(bf16[160,1152]{1,0:T(8,128)(2,1)S(1)} %get-tuple-element.67), channel_id=1, source_target_pairs={{0,1},{1,0},{4,8},{5,9},{8,4},{9,5},{12,13},{13,12},{2,3},{3,2},{6... | collective-permute-start | bytes 1105928 | tf_op jit(solution)/shard_map/ppermute | solution.py:552
  36.5 14.9 %collective-permute-start.8 = (bf16[160,1152]{1,0:T(8,128)(2,1)S(1)}, bf16[160,1152]{1,0:T(8,128)(2,1)S(1)}, u32[]{:S(2)}, u32[]{:S(2)}) collective-permute-start(bf16[160,1152]{1,0:T(8,128)(2,1)S(1)} %get-tuple-element.69), channel_id=1, source_target_pairs={{0,4},{1,5},{4,0},{5,1},{8,12},{9,13},{12,8},{13,9},{2,6},{3,7},{6... | collective-permute-start | bytes 1105928 | tf_op jit(solution)/shard_map/ppermute | solution.py:552
  42.5 12.8 %collective-permute-start.9 = (bf16[160,1152]{1,0:T(8,128)(2,1)S(1)}, bf16[160,1152]{1,0:T(8,128)(2,1)S(1)}, u32[]{:S(2)}, u32[]{:S(2)}) collective-permute-start(bf16[160,1152]{1,0:T(8,128)(2,1)S(1)} %get-tuple-element.73), channel_id=1, source_target_pairs={{0,2},{2,0},{1,3},{3,1},{4,6},{6,4},{5,7},{7,5},{8,10},{10,8},{9,1... | collective-permute-start | bytes 1105928 | tf_op jit(solution)/shard_map/ppermute | solution.py:483
  52.1 12.9 %collective-permute-start.11 = (bf16[160,1152]{1,0:T(8,128)(2,1)S(1)}, bf16[160,1152]{1,0:T(8,128)(2,1)S(1)}, u32[]{:S(2)}, u32[]{:S(2)}) collective-permute-start(bf16[160,1152]{1,0:T(8,128)(2,1)S(1)} %get-tuple-element.76), channel_id=1, source_target_pairs={{0,4},{1,5},{4,0},{5,1},{8,12},{9,13},{12,8},{13,9},{2,6},{3,7},{6... | collective-permute-start | bytes 1105928 | tf_op jit(solution)/shard_map/ppermute | solution.py:552
  55.3 10.1 %collective-permute-start.12 = (bf16[160,1152]{1,0:T(8,128)(2,1)S(1)}, bf16[160,1152]{1,0:T(8,128)(2,1)S(1)}, u32[]{:S(2)}, u32[]{:S(2)}) collective-permute-start(bf16[160,1152]{1,0:T(8,128)(2,1)S(1)} %get-tuple-element.79), channel_id=1, source_target_pairs={{0,1},{1,0},{4,8},{5,9},{8,4},{9,5},{12,13},{13,12},{2,3},{3,2},{6... | collective-permute-start | bytes 1105928 | tf_op jit(solution)/shard_map/ppermute | solution.py:552
  55.3 11.8 %collective-permute-start.15 = (bf16[160,1152]{1,0:T(8,128)(2,1)S(1)}, bf16[160,1152]{1,0:T(8,128)(2,1)S(1)}, u32[]{:S(2)}, u32[]{:S(2)}) collective-permute-start(bf16[160,1152]{1,0:T(8,128)(2,1)S(1)} %get-tuple-element.82.refs_0_), channel_id=1, source_target_pairs={{0,1},{1,0},{2,3},{3,2},{4,5},{5,4},{6,7},{7,6},{8,9},{9,8},{10,11... | collective-permute-start | bytes 1105928 | tf_op jit(solution)/shard_map/ppermute | solution.py:527
  60.5 13.8 %collective-permute-start.16 = (bf16[160,1152]{1,0:T(8,128)(2,1)S(1)}, bf16[160,1152]{1,0:T(8,128)(2,1)S(1)}, u32[]{:S(2)}, u32[]{:S(2)}) collective-permute-start(bf16[160,1152]{1,0:T(8,128)(2,1)S(1)} %collective-permute-done.14.refs_1_), channel_id=1, source_target_pairs={{0,1},{1,0},{2,3},{3,2},{4,5},{5,4},{6,7},{7,6},{8,9},{9,8},{10,11... | collective-permute-start | bytes 1105928 | tf_op jit(solution)/shard_map/ppermute | solution.py:527
  61.0 18.0 %collective-permute-start.13 = (bf16[160,1152]{1,0:T(8,128)(2,1)S(1)}, bf16[160,1152]{1,0:T(8,128)(2,1)S(1)}, u32[]{:S(2)}, u32[]{:S(2)}) collective-permute-start(bf16[160,1152]{1,0:T(8,128)(2,1)S(1)} %get-tuple-element.81), channel_id=1, source_target_pairs={{0,4},{1,5},{4,0},{5,1},{8,12},{9,13},{12,8},{13,9},{2,6},{3,7},{6... | collective-permute-start | bytes 1105928 | tf_op jit(solution)/shard_map/ppermute | solution.py:552
  65.3 13.9 %collective-permute-start.17 = (bf16[160,1152]{1,0:T(8,128)(2,1)S(1)}, bf16[160,1152]{1,0:T(8,128)(2,1)S(1)}, u32[]{:S(2)}, u32[]{:S(2)}) collective-permute-start(bf16[160,1152]{1,0:T(8,128)(2,1)S(1)} %get-tuple-element.85), channel_id=1, source_target_pairs={{0,1},{1,0},{4,8},{5,9},{8,4},{9,5},{12,13},{13,12},{2,3},{3,2},{6... | collective-permute-start | bytes 1105928 | tf_op jit(solution)/shard_map/ppermute | solution.py:552
  65.4 15.9 %collective-permute-start.22 = (bf16[160,1152]{1,0:T(8,128)(2,1)S(1)}, bf16[160,1152]{1,0:T(8,128)(2,1)S(1)}, u32[]{:S(2)}, u32[]{:S(2)}) collective-permute-start(bf16[160,1152]{1,0:T(8,128)(2,1)S(1)} %get-tuple-element.93.refs_0_), channel_id=1, source_target_pairs={{0,2},{2,0},{1,3},{3,1},{4,6},{6,4},{5,7},{7,5},{8,10},{10,8},{9,1... | collective-permute-start | bytes 1105928 | tf_op jit(solution)/shard_map/ppermute | solution.py:524
  67.1 14.8 %collective-permute-start.18 = (bf16[160,1152]{1,0:T(8,128)(2,1)S(1)}, bf16[160,1152]{1,0:T(8,128)(2,1)S(1)}, u32[]{:S(2)}, u32[]{:S(2)}) collective-permute-start(bf16[160,1152]{1,0:T(8,128)(2,1)S(1)} %get-tuple-element.87), channel_id=1, source_target_pairs={{0,4},{1,5},{4,0},{5,1},{8,12},{9,13},{12,8},{13,9},{2,6},{3,7},{6... | collective-permute-start | bytes 1105928 | tf_op jit(solution)/shard_map/ppermute | solution.py:552
  79.3 11.5 %collective-permute-start.20 = (bf16[160,1152]{1,0:T(8,128)(2,1)S(1)}, bf16[160,1152]{1,0:T(8,128)(2,1)S(1)}, u32[]{:S(2)}, u32[]{:S(2)}) collective-permute-start(bf16[160,1152]{1,0:T(8,128)(2,1)S(1)} %get-tuple-element.91), channel_id=1, source_target_pairs={{0,4},{1,5},{4,0},{5,1},{8,12},{9,13},{12,8},{13,9},{2,6},{3,7},{6... | collective-permute-start | bytes 1105928 | tf_op jit(solution)/shard_map/ppermute | solution.py:552
  81.4 9.5 %collective-permute-start.23 = (bf16[160,1152]{1,0:T(8,128)(2,1)S(1)}, bf16[160,1152]{1,0:T(8,128)(2,1)S(1)}, u32[]{:S(2)}, u32[]{:S(2)}) collective-permute-start(bf16[160,1152]{1,0:T(8,128)(2,1)S(1)} %get-tuple-element.93.refs_0_), channel_id=1, source_target_pairs={{0,1},{1,0},{2,3},{3,2},{4,5},{5,4},{6,7},{7,6},{8,9},{9,8},{10,11... | collective-permute-start | bytes 1105928 | tf_op jit(solution)/shard_map/ppermute | solution.py:527
  81.4 9.5 %collective-permute-start.24 = (bf16[160,1152]{1,0:T(8,128)(2,1)S(1)}, bf16[160,1152]{1,0:T(8,128)(2,1)S(1)}, u32[]{:S(2)}, u32[]{:S(2)}) collective-permute-start(bf16[160,1152]{1,0:T(8,128)(2,1)S(1)} %collective-permute-done.22.refs_1_), channel_id=1, source_target_pairs={{0,1},{1,0},{2,3},{3,2},{4,5},{5,4},{6,7},{7,6},{8,9},{9,8},{10,11... | collective-permute-start | bytes 1105928 | tf_op jit(solution)/shard_map/ppermute | solution.py:527
  82.0 13.5 %collective-permute-start.21 = (bf16[160,1152]{1,0:T(8,128)(2,1)S(1)}, bf16[160,1152]{1,0:T(8,128)(2,1)S(1)}, u32[]{:S(2)}, u32[]{:S(2)}) collective-permute-start(bf16[160,1152]{1,0:T(8,128)(2,1)S(1)} %get-tuple-element.92), channel_id=1, source_target_pairs={{0,1},{1,0},{4,8},{5,9},{8,4},{9,5},{12,13},{13,12},{2,3},{3,2},{6... | collective-permute-start | bytes 1105928 | tf_op jit(solution)/shard_map/ppermute | solution.py:552
  82.3 16.4 %collective-permute-start.25 = (bf16[160,1152]{1,0:T(8,128)(2,1)S(1)}, bf16[160,1152]{1,0:T(8,128)(2,1)S(1)}, u32[]{:S(2)}, u32[]{:S(2)}) collective-permute-start(bf16[160,1152]{1,0:T(8,128)(2,1)S(1)} %get-tuple-element.97), channel_id=1, source_target_pairs={{0,4},{1,5},{4,0},{5,1},{8,12},{9,13},{12,8},{13,9},{2,6},{3,7},{6... | collective-permute-start | bytes 1105928 | tf_op jit(solution)/shard_map/ppermute | solution.py:552
  95.7 10.5 %collective-permute-start.26 = (bf16[160,1152]{1,0:T(8,128)(2,1)S(1)}, bf16[160,1152]{1,0:T(8,128)(2,1)S(1)}, u32[]{:S(2)}, u32[]{:S(2)}) collective-permute-start(bf16[160,1152]{1,0:T(8,128)(2,1)S(1)} %get-tuple-element.99), channel_id=1, source_target_pairs={{0,4},{1,5},{4,0},{5,1},{8,12},{9,13},{12,8},{13,9},{2,6},{3,7},{6... | collective-permute-start | bytes 1105928 | tf_op jit(solution)/shard_map/ppermute | solution.py:552
  (13 other events, 75.3 us)
where the time goes:
time: 108 us; the launch traced here: 107 us
  starting transfers between devices  42.3 us (39%)
  Pallas kernels  35.5 us (33%)
  waiting for transfers between devices  24.2 us (22%)
  local copies, waits for them, and re-layouts  4.32 us (4%)
  between operations  1.08 us (1%)
    ppermute x19, starting transfers between devices, body(): lax.ppermute(message, ('edge', 'sys'), swaps(at, edge_size, sys_size))  36.7 us
    ppermute x19, waiting for transfers between devices, body(): lax.ppermute(message, ('edge', 'sys'), swaps(at, edge_size, sys_size))  19.4 us
    pallas_call x2, Pallas kernels, spread(): pl.pallas_call(functools.partial(spread_kernel, count, groups), grid=(row...  9.23 us
    pallas_call x2, Pallas kernels, merge_part(): pl.pallas_call(functools.partial(merge_kernel, expert_size, sys_size, fir...  8.73 us
    ppermute x2, waiting for transfers between devices, finish(): column.append(lax.ppermute(rows_h, 'expert', shift(expert_size, k)))  4.74 us
    unnamed x20, local copies, waits for them, and re-layouts  4.32 us
    pallas_call x1, Pallas kernels, input_product(): pl.pallas_call(functools.partial(input_kernel, sys_size), grid=(width_in...  4.24 us
    pallas_call x1, Pallas kernels, outer_products(): pl.pallas_call(functools.partial(outer_kernel, sys_size), grid=(width_in...  3.84 us
  transfers between devices with their start and end apart: 27, of which 8 were waited for; matrix products, arithmetic and copies ran while one was open for 0% of the time, Pallas kernels for 28%

commit v1 on v0

--- a/solution.py
+++ b/solution.py
@@ -9,18 +9,22 @@
 from jax.sharding import PartitionSpec as P
 
 
-LAG, EVEN_LAG, ODD_LAG = 3, 3, 3
+LAG = 3
+SPLIT = ()
+SKIPPED = (4,)
+SUMS_FIRST, SUMS_CHUNK, ROWS_CHUNK, OWN_WEIGHT = 3, 1, 0, -0.7
 MERGED_AT = (6, 8)
-SPREAD_BEFORE = (15, 20)
-MIX_BEFORE = 8
+SPREAD_BEFORE = (17, 99)
+MIX_BEFORE = 12
 ENDS_GRANT = 62 << 20
+MERGES_TOGETHER = True
 
 
 def entry(values, at):
     return values[min(at, len(values) - 1)] + 4 * max(0, at - len(values) + 1)
 
 
-def plan(size, chunks):
+def plan(size, chunks, halves):
     sums = {}
     rows = {}
     for h in range(chunks):
@@ -36,7 +40,7 @@
     while len(sent) < total:
         at = len(steps)
         step = []
-        for low in range(at % 2, size - 1, 2):
+        for low in range(at % 2, 0 if at in SKIPPED else size - 1, 2):
             for source, way in ((low, 1), (low + 1, -1)):
                 target = source + way
                 left = size - 1 - target if way == 1 else target
@@ -44,17 +48,18 @@
                 for h in range(chunks):
                     for b in range(size):
                         ahead = (b - target) * way
+                        own = OWN_WEIGHT if b == source else 0
                         for kind, state, order in (
-                            ("S", sums.get((source, way, b, h)) if ahead >= 0 else None, (-ahead - 2, 0, h)),
-                            ("M", rows.get((source, b, h)) if (source - b) * way >= 0 else None, (-left, 1, h)),
+                            ("S", sums.get((source, way, b, h)) if ahead >= 0 else None, SUMS_CHUNK * h - ahead - SUMS_FIRST),
+                            ("M", rows.get((source, b, h)) if (source - b) * way >= 0 else None, ROWS_CHUNK * h - left + own),
                         ):
                             if state and state[0] <= at and (kind, source, way, b, h) not in sent:
-                                ready.append(((state[1] > at, *order), (kind, b, h), state[2]))
+                                ready.append(((state[1] > at, order, kind != "S", h), (kind, b, h), state[2]))
                 if ready:
                     _, (kind, b, h), came = min(ready, key=lambda choice: choice[0])
                     sent.add((kind, source, way, b, h))
                     step.append((source, target, kind, b, h, came))
-        lag = ODD_LAG if at % 2 else EVEN_LAG
+        lag = 1 if halves and at % 2 and at in SPLIT else LAG
         for source, target, kind, b, h, _ in step:
             if kind == "M":
                 rows[target, b, h] = (at + lag, at + LAG, at)
@@ -62,6 +67,16 @@
                 sums[target, target - source, b, h] = (at + lag, at + LAG, at)
         steps.append(step)
     return steps
+
+
+def parts_of(at, halves):
+    return (0, 1) if halves and at in SPLIT else (None,)
+
+
+def layout(row_count):
+    chunks = 2 if row_count % 32 == 0 else 1
+    rows = row_count // chunks
+    return chunks, rows, rows % 32 == 0
 
 
 def at_device(values):
@@ -138,7 +153,7 @@
     return jnp.where(at < live, grad_ref[...], jnp.zeros((), grad_ref.dtype))
 
 
-def ends_kernel(sys_size, rows, starts, span, counts_ref, features_ref, grad_ref, *refs):
+def ends_kernel(sys_size, pieces, starts, span, counts_ref, features_ref, grad_ref, *refs):
     outs, (features, grad, product, ready) = refs[:-4], refs[-4:]
     lanes = features.shape[1]
     first = at_device(starts)
@@ -157,25 +172,27 @@
         (((0,), (0,)), ((), ())),
         preferred_element_type=jnp.float32,
     ).astype(product.dtype)
-    for h, out_ref in enumerate(outs):
-        out_ref[...] = product[pl.ds(pl.multiple_of(first - window + h * rows, 16), rows), :]
-
-
-def end_products(counts, features, grad, sys_size, edge_size, chunks, rows):
+    for (start, rows), out_ref in zip(pieces, outs):
+        out_ref[...] = product[pl.ds(pl.multiple_of(first - window + start, 16), rows), :]
+
+
+def end_products(counts, features, grad, sys_size, edge_size, block, pieces):
     edges, width_in = features.shape
     width = grad.shape[1]
-    block = chunks * rows
-    starts = [0 if z else (edge_size - 1) * block for z in range(edge_size)]
-    lanes = max(-(-(one % 128 + block) // 128) * 128 for one in starts)
-    return pl.pallas_call(
-        functools.partial(ends_kernel, sys_size, rows, starts, width_in),
+    base = min(start for start, _ in pieces)
+    extent = max(start + rows for start, rows in pieces) - base
+    starts = [base + (0 if z else (edge_size - 1) * block) for z in range(edge_size)]
+    lanes = min(width_in, max(-(-(one % 128 + extent) // 128) * 128 for one in starts))
+    pieces = [(start - base, rows) for start, rows in pieces]
+    return pl.pallas_call(
+        functools.partial(ends_kernel, sys_size, pieces, starts, width_in),
         in_specs=[
             pl.BlockSpec(memory_space=pltpu.SMEM),
             pl.BlockSpec(memory_space=pl.ANY),
             pl.BlockSpec(memory_space=pl.ANY),
         ],
-        out_specs=[pl.BlockSpec(memory_space=pltpu.VMEM)] * chunks,
-        out_shape=[jax.ShapeDtypeStruct((rows, width), jnp.bfloat16)] * chunks,
+        out_specs=[pl.BlockSpec(memory_space=pltpu.VMEM)] * len(pieces),
+        out_shape=[jax.ShapeDtypeStruct((rows, width), jnp.bfloat16) for _, rows in pieces],
         scratch_shapes=[
             pltpu.VMEM((edges, lanes), jnp.bfloat16),
             pltpu.VMEM((edges, width), jnp.bfloat16),
@@ -190,13 +207,13 @@
     )(counts, features, grad)
 
 
-def outer_kernel(sys_size, counts_ref, features_ref, grad_ref, out_ref, masked):
+def outer_kernel(sys_size, counts_ref, features_ref, grad_ref, out_ref, live_ref):
     @pl.when(pl.program_id(0) == 0)
     def _():
-        masked[...] = live_rows(grad_ref, counts_ref, sys_size)
+        live_ref[...] = live_rows(grad_ref, counts_ref, sys_size)
 
     out_ref[...] = lax.dot_general(
-        features_ref[...], masked[...], (((0,), (0,)), ((), ())), preferred_element_type=jnp.float32
+        features_ref[...], live_ref[...], (((0,), (0,)), ((), ())), preferred_element_type=jnp.float32
     ).astype(out_ref.dtype)
 
 
@@ -212,9 +229,14 @@
             pl.BlockSpec((edges, tile), lambda i: (0, i)),
             pl.BlockSpec((edges, width), lambda i: (0, 0)),
         ],
-        out_specs=pl.BlockSpec((tile, width), lambda i: (i, 0)),
-        out_shape=jax.ShapeDtypeStruct((store_rows, width), jnp.bfloat16),
-        scratch_shapes=[pltpu.VMEM((edges, width), jnp.bfloat16)],
+        out_specs=[
+            pl.BlockSpec((tile, width), lambda i: (i, 0)),
+            pl.BlockSpec((edges, width), lambda i: (0, 0)),
+        ],
+        out_shape=[
+            jax.ShapeDtypeStruct((store_rows, width), jnp.bfloat16),
+            jax.ShapeDtypeStruct((edges, width), jnp.bfloat16),
+        ],
         compiler_params=pltpu.CompilerParams(vmem_limit_bytes=12 << 20),
         cost_estimate=pl.CostEstimate(
             flops=2 * edges * width_in * width,
@@ -225,35 +247,24 @@
     )(counts, features, grad)
 
 
-def input_kernel(sys_size, counts_ref, grad_ref, rows_ref, out_ref, live_ref):
-    @pl.when(pl.program_id(0) == 0)
-    def _():
-        live_ref[...] = live_rows(grad_ref, counts_ref, sys_size)
-
+def input_kernel(live_ref, rows_ref, out_ref):
     out_ref[...] = lax.dot_general(
         live_ref[...], rows_ref[...], (((1,), (1,)), ((), ())), preferred_element_type=jnp.float32
     ).astype(out_ref.dtype)
 
 
-def input_product(counts, grad, store, sys_size, width_in):
-    edges, width = grad.shape
+def input_product(live, store, width_in):
+    edges, width = live.shape
     tile = 256 if width_in % 256 == 0 else width_in
     return pl.pallas_call(
-        functools.partial(input_kernel, sys_size),
+        input_kernel,
         grid=(width_in // tile,),
         in_specs=[
-            pl.BlockSpec(memory_space=pltpu.SMEM),
             pl.BlockSpec((edges, width), lambda i: (0, 0)),
             pl.BlockSpec((tile, width), lambda i: (width_in // tile + i, 0)),
         ],
-        out_specs=[
-            pl.BlockSpec((edges, tile), lambda i: (0, i)),
-            pl.BlockSpec((edges, width), lambda i: (0, 0)),
-        ],
-        out_shape=[
-            jax.ShapeDtypeStruct((edges, width_in), jnp.bfloat16),
-            jax.ShapeDtypeStruct((edges, width), jnp.bfloat16),
-        ],
+        out_specs=pl.BlockSpec((edges, tile), lambda i: (0, i)),
+        out_shape=jax.ShapeDtypeStruct((edges, width_in), jnp.bfloat16),
         compiler_params=pltpu.CompilerParams(vmem_limit_bytes=12 << 20),
         cost_estimate=pl.CostEstimate(
             flops=2 * edges * width_in * width,
@@ -261,7 +272,7 @@
             transcendentals=0,
         ),
         name="input_product",
-    )(counts, grad, store)
+    )(live, store)
 
 
 def last_kernel(width_in, windows, live_ref, store_ref, _, out_ref, part, done):
@@ -298,15 +309,11 @@
     )(live, store, product)
 
 
-def hop_kernel(count, behind, take, add, send, rows, *refs):
+def hop_kernel(count, behind, take, add, origin, *refs):
     arrays, (store, *message) = refs[1 : 1 + count], refs[1 + count + behind :]
     if count:
-        into = at_device(take) * rows
+        into = at_device(take)
         adds = at_device(add) == 1
-    if send is not None:
-        origin = at_device(send) * rows
-
-    if count:
 
         def update(i, _):
             span = pl.ds(pl.multiple_of(i * 16, 16), 16)
@@ -318,25 +325,27 @@
             store[here, :] = total.astype(store.dtype)
             return 0
 
-        lax.fori_loop(0, rows // 16, update, 0)
-    if send is not None:
+        lax.fori_loop(0, arrays[0].shape[0] // 16, update, 0)
+    if message:
+        out = message[0]
+        first = at_device(origin)
 
         def copy(i, _):
             span = pl.ds(pl.multiple_of(i * 16, 16), 16)
-            message[0][span, :] = store[pl.ds(pl.multiple_of(origin + i * 16, 16), 16), :]
+            out[span, :] = store[pl.ds(pl.multiple_of(first + i * 16, 16), 16), :]
             return 0
 
-        lax.fori_loop(0, rows // 16, copy, 0)
-
-
-def hop(store, arrays, take, add, send, rows, behind=()):
+        lax.fori_loop(0, out.shape[0] // 16, copy, 0)
+
+
+def hop(store, arrays, take, add, origin, rows, behind=()):
     width = store.shape[1]
     vmem = pl.BlockSpec(memory_space=pltpu.VMEM)
     shapes = [jax.ShapeDtypeStruct(store.shape, store.dtype)]
-    if send is not None:
+    if origin is not None:
         shapes.append(jax.ShapeDtypeStruct((rows, width), store.dtype))
     return pl.pallas_call(
-        functools.partial(hop_kernel, len(arrays), len(behind), take, add, send, rows),
+        functools.partial(hop_kernel, len(arrays), len(behind), take, add, origin),
         in_specs=[vmem] * (1 + len(arrays)) + [pl.BlockSpec(memory_space=pl.ANY)] * len(behind),
         out_specs=[vmem] * len(shapes),
         out_shape=shapes,
@@ -451,10 +460,6 @@
     return [(i, (i + by) % size) for i in range(size)]
 
 
-def chunks_of(row_count):
-    return 2 if row_count % 32 == 0 else 1
-
-
 def body(edge_inputs, out_grad, expert_weights, coef_table, system_kind, edge_counts):
     edge_size = lax.axis_size("edge")
     expert_size = lax.axis_size("expert")
@@ -462,18 +467,29 @@
     exp_local, row_count, _ = expert_weights.shape
     width_in = edge_inputs.shape[2]
     edge_rows = out_grad.shape[1]
-    chunks = chunks_of(row_count)
-    rows = row_count // chunks
+    chunks, rows, halves = layout(row_count)
+    half = rows // 2
     tile = 32 if rows % 32 == 0 else 16
     features, grad = edge_inputs[0], out_grad[0]
     places = edge_size * chunks
-    spare = 2 * places
 
     scale = 1.0 / math.sqrt(edge_rows * edge_size)
     mix = mix_matrix(coef_table, system_kind, expert_size, sys_size, exp_local, scale, tile)
 
-    firsts = end_products(edge_counts, features, grad, sys_size, edge_size, chunks, rows)
-    store = outer_products(edge_counts, features, grad, sys_size, (2 * places + 1) * rows)
+    steps = plan(edge_size, chunks, halves)
+    moves = [(at, part) for at, step in enumerate(steps) if step for part in parts_of(at, halves)]
+
+    def extent(h, part):
+        return (h * rows, rows) if part is None else (h * rows + part * half, half)
+
+    def from_ends(at):
+        far = all(b == (0 if source else edge_size - 1) for source, _, _, b, _, _ in steps[at])
+        return far and all(kind == "S" and came is None for _, _, kind, _, _, came in steps[at])
+
+    early = [(at, part) for at, part in moves if from_ends(at)]
+    pieces = [extent(steps[at][0][4], part) for at, part in early]
+    firsts = dict(zip(early, end_products(edge_counts, features, grad, sys_size, edge_size, row_count, pieces)))
+    store, live = outer_products(edge_counts, features, grad, sys_size, (2 * places + 1) * rows)
     exchanged = []
     for h in range(chunks):
         parts = merge_part(
@@ -483,7 +499,6 @@
         arrays += [lax.ppermute(parts[k], "expert", shift(expert_size, k)) for k in range(1, expert_size)]
         exchanged.append(arrays)
 
-    steps = plan(edge_size, chunks)
     pending = []
     got = {}
     merged = set()
@@ -492,19 +507,24 @@
     result = None
 
     def own(first):
-        return [first + z * chunks for z in range(edge_size)]
-
-    def settle(store, at, origin, behind=()):
-        take, add = [spare] * edge_size, [0] * edge_size
+        return [first + z * row_count for z in range(edge_size)]
+
+    def row_at(kind, b):
+        return b * row_count + (width_in if kind == "M" else 0)
+
+    def settle(store, move, origin, count, behind=()):
+        at, part = move
+        take, add = [2 * width_in] * edge_size, [0] * edge_size
         for _, target, kind, b, h, _ in steps[at]:
-            take[target] = b * chunks + h + (places if kind == "M" else 0)
+            take[target] = row_at(kind, b) + extent(h, part)[0]
             add[target] = int(kind == "S")
             if kind == "S" and b == target:
-                waiting[h] -= 1
-        pending.remove(at)
-        return hop(store, [got.pop(at)], take, add, origin, rows, behind)
+                waiting[h] -= 1 if part is None else 0.5
+        pending.remove(move)
+        return hop(store, [got.pop(move)], take, add, origin, count, behind)
 
     tokens = {}
+
     mixed = [mix]
 
     def overdue(at):
@@ -518,7 +538,7 @@
             if waiting[h] or h in taken:
                 continue
             taken.add(h)
-            store, rows_h = hop(store, [], None, None, own(h), rows)
+            store, rows_h = hop(store, [], None, None, own(h * rows), rows)
             column = [rows_h]
             for k in range(1, expert_size):
                 column.append(lax.ppermute(rows_h, "expert", shift(expert_size, k)))
@@ -529,38 +549,60 @@
             tokens[h] = token
         return store, result
 
-    for at, step in enumerate(steps):
-        if not step:
-            continue
+    used = [at for at, step in enumerate(steps) if step]
+    last, first_of_last = {}, used[-1]
+    for at in reversed(used[-2:]):
+        new = {target: b * chunks + h for _, target, kind, b, h, _ in steps[at] if kind == "M"}
+        if set(new) & set(last):
+            break
+        last.update(new)
+        first_of_last = at
+    product = None
+
+    def whole_product(store):
+        return input_product(live, store, width_in)
+
+    for move in moves:
+        at, part = move
+        step = steps[at]
         for source, _, kind, b, h, _ in step:
             if kind == "M" and b == source and h not in merged:
                 merged.add(h)
-                (store,) = hop(store, exchanged[h], own(places + h), [0] * edge_size, None, rows)
-        origin = [spare] * edge_size
-        for source, _, kind, b, h, _ in step:
-            origin[source] = b * chunks + h + (places if kind == "M" else 0)
-        needed = {came for *_, came in step}
-        due = [one for one in pending if one in needed or one <= at - LAG]
-        for one in due[:-1]:
-            (store,) = settle(store, one, None)
-        if all((kind, b) == ("S", 0 if source else edge_size - 1) and came is None for source, _, kind, b, _, came in step):
-            message = firsts[step[0][4]]
-        elif due:
-            store, message = settle(store, due[-1], origin, overdue(at))
-        else:
-            store, message = hop(store, [], None, None, origin, rows, overdue(at))
-        got[at] = lax.ppermute(message, ("edge", "sys"), swaps(at, edge_size, sys_size))
-        pending.append(at)
+                behind = [exchanged[1][0]] if chunks > 1 and MERGES_TOGETHER else []
+                (store,) = hop(store, exchanged[h], own(width_in + h * rows), [0] * edge_size, None, rows, behind)
+        origin, count, needed = [2 * width_in] * edge_size, None, set()
+        for source, _, kind, b, h, came in step:
+            first, count = extent(h, part)
+            origin[source] = row_at(kind, b) + first
+            if came is not None:
+                brought = parts_of(came, halves)
+                needed |= {(came, one) for one in brought if part is None or one is None or one == part}
+        due = [one for one in pending if one in needed or one[0] <= at - LAG]
+        for one in due:
+            waits = one[0] >= first_of_last
+            if waits and product is None:
+                product = whole_product(store)
+            behind = overdue(at) + ([product] if waits else [])
+            if one == due[-1]:
+                store, message = settle(store, one, origin, count, behind)
+            else:
+                (store,) = settle(store, one, None, rows, behind)
+                store, result = finish(store, result)
+        if move in firsts:
+            message = firsts[move]
+        elif not due:
+            store, message = hop(store, [], None, None, origin, count, overdue(at))
+        got[move] = lax.ppermute(message, ("edge", "sys"), swaps(at, edge_size, sys_size))
+        pending.append(move)
         store, result = finish(store, result)
-    while len(pending) > 1:
-        (store,) = settle(store, pending[0], None, list(tokens.values()) if len(pending) == 2 else ())
+    while pending:
+        waits = pending[0][0] >= first_of_last
+        if waits and product is None:
+            product = whole_product(store)
+        behind = (list(tokens.values()) if len(pending) == 1 else []) + ([product] if waits else [])
+        (store,) = settle(store, pending[0], None, rows, behind)
         store, result = finish(store, result)
-    product, live = input_product(edge_counts, grad, store, sys_size, width_in)
-    last = [0] * edge_size
-    for _, target, _, b, h, _ in steps[pending[0]]:
-        last[target] = b * chunks + h
-    (store,) = settle(store, pending[0], None, (live,))
-    store, result = finish(store, result)
+    last = [last.get(z, 0) for z in range(edge_size)]
     input_grad = last_product(live, store, product, rows, last)
     return (input_grad[None], result)
 

time: 108 us -> 103 us (0.954)
  starting transfers between devices: 42.3 us -> 37.2 us
    ppermute x19 -> x18, starting transfers between devices: 36.7 us -> 32.2 us  [body(): lax.ppermute(message, ('edge', 'sys'), swaps(at, edge_size, sys_size))]
    unnamed x20 -> x14, local copies, waits for them, and re-layouts: 4.32 us -> 5.15 us
    ppermute x19 -> x18, waiting for transfers between devices: 19.4 us -> 19 us  [body(): lax.ppermute(message, ('edge', 'sys'), swaps(at, edge_size, sys_size))]
  transfers between devices with their start and end apart: 27 -> 26, of which waited for: 8 -> 9; matrix products, arithmetic and copies ran while one was open for 0% -> 0% of each run, Pallas kernels for 28% -> 29%
where the time goes in v1:
time: 103 us
  starting transfers between devices  37.2 us (36%)
  Pallas kernels  34.6 us (34%)
  waiting for transfers between devices  24.6 us (24%)
  local copies, waits for them, and re-layouts  5.15 us (5%)
    ppermute x18, starting transfers between devices, body(): lax.ppermute(message, ('edge', 'sys'), swaps(at, edge_size, sys_size))  32.2 us
    ppermute x18, waiting for transfers between devices, body(): lax.ppermute(message, ('edge', 'sys'), swaps(at, edge_size, sys_size))  19 us
    pallas_call x2, Pallas kernels, spread(): pl.pallas_call(functools.partial(spread_kernel, count, groups), grid=(row...  9.22 us
    pallas_call x2, Pallas kernels, merge_part(): pl.pallas_call(functools.partial(merge_kernel, expert_size, sys_size, fir...  8.73 us
    ppermute x2, waiting for transfers between devices, finish(): column.append(lax.ppermute(rows_h, 'expert', shift(expert_size, k)))  5.65 us
    unnamed x14, local copies, waits for them, and re-layouts  5.15 us
    pallas_call x24, Pallas kernels, hop(): pl.pallas_call(functools.partial(hop_kernel, len(arrays), len(behind), ta...  3.9 us
    pallas_call x1, Pallas kernels, outer_products(): pl.pallas_call(functools.partial(outer_kernel, sys_size), grid=(width_in...  3.87 us
  transfers between devices with their start and end apart: 26, of which 9 were waited for; matrix products, arithmetic and copies ran while one was open for 0% of the time, Pallas kernels for 29%

profile of v1, /device:TPU:0, one launch (start us, length us, event | category | flops | bytes accessed | tf_op | source)
XLA Modules:
  0.0 102.6 jit_solution(4071807700631459822)
XLA Ops:
  0.6 3.3 %ends.1 = bf16[160,1152]{1,0:T(8,128)(2,1)} custom-call(s32[4]{0:T(128)} %counts_ref.3, bf16[448,1280]{1,0:T(8,128)(2,1)} %bitcast.4, bf16[448,1152]{1,0:T(8,128)(2,1)} %bitcast.6), custom_call_target="tpu_custom_call" | custom-call | flops 264241152 | bytes 1261568 | tf_op jit(solution)/shard_map/ends/pallas_call | solution.py:187
  3.9 3.1 %collective-permute-start = (bf16[160,1152]{1,0:T(8,128)(2,1)}, bf16[160,1152]{1,0:T(8,128)(2,1)S(1)}, u32[]{:S(2)}, u32[]{:S(2)}) collective-permute-start(bf16[160,1152]{1,0:T(8,128)(2,1)} %ends.1), channel_id=1, source_target_pairs={{0,4},{1,5},{4,0},{5,1},{8,12},{9,13},{12,8},{13,9},{2,6},{3,7},{6... | collective-permute-start | bytes 1105928 | tf_op jit(solution)/shard_map/ppermute | solution.py:595
  10.1 3.9 %outer.1 = (bf16[2720,1152]{1,0:T(8,128)(2,1)S(1)}, bf16[448,1152]{1,0:T(8,128)(2,1)S(1)}) custom-call(s32[4]{0:T(128)S(1)} %copy-done.6, bf16[448,1280]{1,0:T(8,128)(2,1)S(1)} %bitcast.5, bf16[448,1152]{1,0:T(8,128)(2,1)S(1)} %bitcast.7), custom_call_target="tpu_custom_call" | custom-call | flops 1321205760 | bytes 5128192 | tf_op jit(solution)/shard_map/outer/pallas_call | solution.py:224
  14.2 1.8 %collective-permute-done.refs_1_ = bf16[160,1152]{1,0:T(8,128)(2,1)S(1)} collective-permute-done((bf16[160,1152]{1,0:T(8,128)(2,1)}, bf16[160,1152]{1,0:T(8,128)(2,1)S(1)}, u32[]{:S(2)}, u32[]{:S(2)}) %collective-permute-start) | collective-permute-done | bytes 368672 | tf_op jit(solution)/shard_map/ppermute | solution.py:595
  16.4 2.0 %copy-done = bf16[16,320,1152]{2,1,0:T(8,128)(2,1)S(1)} copy-done((bf16[16,320,1152]{2,1,0:T(8,128)(2,1)S(1)}, bf16[16,320,1152]{2,1,0:T(8,128)(2,1)}, u32[]{:S(2)}) %copy-start) | copy-done | bytes 11796504
  18.4 4.4 %merge.2 = (bf16[160,1152]{1,0:T(8,128)(2,1)S(1)}, bf16[160,1152]{1,0:T(8,128)(2,1)S(1)}) custom-call(f32[16,32]{1,0:T(8,128)S(1)} %copy-done.4, s32[4]{0:T(128)S(1)} %copy-done.5, bf16[16,320,1152]{2,1,0:T(8,128)(2,1)S(1)} %copy-done), custom_call_target="tpu_custom_call" | custom-call | flops 11796480 | bytes 5898240 | tf_op jit(solution)/shard_map/merge/pallas_call | solution.py:130
  22.7 1.6 %collective-permute-start.3 = (bf16[160,1152]{1,0:T(8,128)(2,1)S(1)}, bf16[160,1152]{1,0:T(8,128)(2,1)S(1)}, u32[]{:S(2)}, u32[]{:S(2)}) collective-permute-start(bf16[160,1152]{1,0:T(8,128)(2,1)S(1)} %get-tuple-element.59), channel_id=1, source_target_pairs={{0,2},{2,0},{1,3},{3,1},{4,6},{6,4},{5,7},{7,5},{8,10},{10,8},{9,1... | collective-permute-start | bytes 1105928 | tf_op jit(solution)/shard_map/ppermute | solution.py:499
  24.6 4.4 %merge.3 = (bf16[160,1152]{1,0:T(8,128)(2,1)S(1)}, bf16[160,1152]{1,0:T(8,128)(2,1)S(1)}) custom-call(f32[16,32]{1,0:T(8,128)S(1)} %copy-done.4, s32[4]{0:T(128)S(1)} %copy-done.5, bf16[16,320,1152]{2,1,0:T(8,128)(2,1)S(1)} %copy-done), custom_call_target="tpu_custom_call" | custom-call | flops 11796480 | bytes 5898240 | tf_op jit(solution)/shard_map/merge/pallas_call | solution.py:130
  30.7 3.2 %collective-permute-start.5 = (bf16[160,1152]{1,0:T(8,128)(2,1)S(1)}, bf16[160,1152]{1,0:T(8,128)(2,1)S(1)}, u32[]{:S(2)}, u32[]{:S(2)}) collective-permute-start(bf16[160,1152]{1,0:T(8,128)(2,1)S(1)} %get-tuple-element.64), channel_id=1, source_target_pairs={{0,4},{1,5},{4,0},{5,1},{8,12},{9,13},{12,8},{13,9},{2,6},{3,7},{6... | collective-permute-start | bytes 1105928 | tf_op jit(solution)/shard_map/ppermute | solution.py:595
  34.5 3.5 %collective-permute-start.8 = (bf16[160,1152]{1,0:T(8,128)(2,1)S(1)}, bf16[160,1152]{1,0:T(8,128)(2,1)S(1)}, u32[]{:S(2)}, u32[]{:S(2)}) collective-permute-start(bf16[160,1152]{1,0:T(8,128)(2,1)S(1)} %get-tuple-element.69), channel_id=1, source_target_pairs={{0,4},{1,5},{4,0},{5,1},{8,12},{9,13},{12,8},{13,9},{2,6},{3,7},{6... | collective-permute-start | bytes 1105928 | tf_op jit(solution)/shard_map/ppermute | solution.py:595
  38.0 5.4 %collective-permute-done.5.refs_1_ = bf16[160,1152]{1,0:T(8,128)(2,1)S(1)} collective-permute-done((bf16[160,1152]{1,0:T(8,128)(2,1)S(1)}, bf16[160,1152]{1,0:T(8,128)(2,1)S(1)}, u32[]{:S(2)}, u32[]{:S(2)}) %collective-permute-start.5) | collective-permute-done | bytes 368672 | tf_op jit(solution)/shard_map/ppermute | solution.py:595
  44.0 2.1 %collective-permute-start.10 = (bf16[160,1152]{1,0:T(8,128)(2,1)S(1)}, bf16[160,1152]{1,0:T(8,128)(2,1)S(1)}, u32[]{:S(2)}, u32[]{:S(2)}) collective-permute-start(bf16[160,1152]{1,0:T(8,128)(2,1)S(1)} %get-tuple-element.74), channel_id=1, source_target_pairs={{0,4},{1,5},{4,0},{5,1},{8,12},{9,13},{12,8},{13,9},{2,6},{3,7},{6... | collective-permute-start | bytes 1105928 | tf_op jit(solution)/shard_map/ppermute | solution.py:595
  46.1 5.2 %collective-permute-done.8.refs_1_ = bf16[160,1152]{1,0:T(8,128)(2,1)S(1)} collective-permute-done((bf16[160,1152]{1,0:T(8,128)(2,1)S(1)}, bf16[160,1152]{1,0:T(8,128)(2,1)S(1)}, u32[]{:S(2)}, u32[]{:S(2)}) %collective-permute-start.8) | collective-permute-done | bytes 368672 | tf_op jit(solution)/shard_map/ppermute | solution.py:595
  53.4 2.1 %collective-permute-start.12 = (bf16[160,1152]{1,0:T(8,128)(2,1)S(1)}, bf16[160,1152]{1,0:T(8,128)(2,1)S(1)}, u32[]{:S(2)}, u32[]{:S(2)}) collective-permute-start(bf16[160,1152]{1,0:T(8,128)(2,1)S(1)} %get-tuple-element.78), channel_id=1, source_target_pairs={{0,4},{1,5},{4,0},{5,1},{8,12},{9,13},{12,8},{13,9},{2,6},{3,7},{6... | collective-permute-start | bytes 1105928 | tf_op jit(solution)/shard_map/ppermute | solution.py:595
  55.5 2.6 %collective-permute-done.10.refs_1_ = bf16[160,1152]{1,0:T(8,128)(2,1)S(1)} collective-permute-done((bf16[160,1152]{1,0:T(8,128)(2,1)S(1)}, bf16[160,1152]{1,0:T(8,128)(2,1)S(1)}, u32[]{:S(2)}, u32[]{:S(2)}) %collective-permute-start.10) | collective-permute-done | bytes 368672 | tf_op jit(solution)/shard_map/ppermute | solution.py:595
  59.3 6.4 %collective-permute-start.14 = (bf16[160,1152]{1,0:T(8,128)(2,1)S(1)}, bf16[160,1152]{1,0:T(8,128)(2,1)S(1)}, u32[]{:S(2)}, u32[]{:S(2)}) collective-permute-start(bf16[160,1152]{1,0:T(8,128)(2,1)S(1)} %get-tuple-element.82), channel_id=1, source_target_pairs={{0,4},{1,5},{4,0},{5,1},{8,12},{9,13},{12,8},{13,9},{2,6},{3,7},{6... | collective-permute-start | bytes 1105928 | tf_op jit(solution)/shard_map/ppermute | solution.py:595
  66.6 7.1 %collective-permute-start.19 = (bf16[160,1152]{1,0:T(8,128)(2,1)S(1)}, bf16[160,1152]{1,0:T(8,128)(2,1)S(1)}, u32[]{:S(2)}, u32[]{:S(2)}) collective-permute-start(bf16[160,1152]{1,0:T(8,128)(2,1)S(1)} %get-tuple-element.88), channel_id=1, source_target_pairs={{0,4},{1,5},{4,0},{5,1},{8,12},{9,13},{12,8},{13,9},{2,6},{3,7},{6... | collective-permute-start | bytes 1105928 | tf_op jit(solution)/shard_map/ppermute | solution.py:595
  73.7 4.6 %spread.2 = (bf16[16,320,1152]{2,1,0:T(8,128)(2,1)}, f32[8,128]{1,0:T(8,128)S(1)}) custom-call(bf16[512,256]{1,0:T(8,128)(2,1)S(1)} %mix.1.refs_2_.mix_ref, bf16[160,1152]{1,0:T(8,128)(2,1)S(1)} %get-tuple-element.83.refs_0_, bf16[160,1152]{1,0:T(8,128)(2,1)S(1)} %collective-permute-done.15.refs_1_, bf16[160,1152]{1,0:T(8,128)(2,1)S(1)} %collective-permute-done.16.refs_2_, ...), custom_call_target="tpu_custom_call" | custom-call | flops 1509949440 | bytes 5898240 | tf_op jit(solution)/shard_map/spread/pallas_call | solution.py:426
  78.6 2.4 %collective-permute-done.19.refs_1_ = bf16[160,1152]{1,0:T(8,128)(2,1)S(1)} collective-permute-done((bf16[160,1152]{1,0:T(8,128)(2,1)S(1)}, bf16[160,1152]{1,0:T(8,128)(2,1)S(1)}, u32[]{:S(2)}, u32[]{:S(2)}) %collective-permute-start.19) | collective-permute-done | bytes 368672 | tf_op jit(solution)/shard_map/ppermute | solution.py:595
  82.0 2.5 %collective-permute-start.21 = (bf16[160,1152]{1,0:T(8,128)(2,1)S(1)}, bf16[160,1152]{1,0:T(8,128)(2,1)S(1)}, u32[]{:S(2)}, u32[]{:S(2)}) collective-permute-start(bf16[160,1152]{1,0:T(8,128)(2,1)S(1)} %get-tuple-element.92), channel_id=1, source_target_pairs={{0,4},{1,5},{4,0},{5,1},{8,12},{9,13},{12,8},{13,9},{2,6},{3,7},{6... | collective-permute-start | bytes 1105928 | tf_op jit(solution)/shard_map/ppermute | solution.py:595
  84.5 5.4 %collective-permute-done.23.refs_1_ = bf16[160,1152]{1,0:T(8,128)(2,1)S(1)} collective-permute-done((bf16[160,1152]{1,0:T(8,128)(2,1)S(1)}, bf16[160,1152]{1,0:T(8,128)(2,1)S(1)}, u32[]{:S(2)}, u32[]{:S(2)}) %collective-permute-start.23) | collective-permute-done | bytes 368672 | tf_op jit(solution)/shard_map/ppermute | solution.py:544
  90.0 1.7 %collective-permute-start.22 = (bf16[160,1152]{1,0:T(8,128)(2,1)S(1)}, bf16[160,1152]{1,0:T(8,128)(2,1)S(1)}, u32[]{:S(2)}, u32[]{:S(2)}) collective-permute-start(bf16[160,1152]{1,0:T(8,128)(2,1)S(1)} %get-tuple-element.93), channel_id=1, source_target_pairs={{0,4},{1,5},{4,0},{5,1},{8,12},{9,13},{12,8},{13,9},{2,6},{3,7},{6... | collective-permute-start | bytes 1105928 | tf_op jit(solution)/shard_map/ppermute | solution.py:595
  93.1 3.6 %input_product.1.refs_3_._ = bf16[448,1280]{1,0:T(8,128)(2,1)} custom-call(bf16[448,1152]{1,0:T(8,128)(2,1)S(1)} %get-tuple-element.50.live_ref, bf16[2720,1152]{1,0:T(8,128)(2,1)S(1)} %hop.46.rows_ref.refs_0_), custom_call_target="tpu_custom_call" | custom-call | flops 1321205760 | bytes 5128192 | tf_op jit(solution)/shard_map/input_product/pallas_call | solution.py:259
  96.7 4.6 %spread.3 = (bf16[16,320,1152]{2,1,0:T(8,128)(2,1)}, f32[8,128]{1,0:T(8,128)S(1)}) custom-call(bf16[512,256]{1,0:T(8,128)(2,1)S(1)} %mix.1.refs_2_.mix_ref, bf16[160,1152]{1,0:T(8,128)(2,1)S(1)} %get-tuple-element.94.refs_0_, bf16[160,1152]{1,0:T(8,128)(2,1)S(1)} %collective-permute-done.23.refs_1_, ...), custom_call_target="tpu_custom_call", output_to_operand_aliasing={{0}: (5, {})} | custom-call | flops 1509949440 | bytes 5898240 | tf_op jit(solution)/shard_map/spread/pallas_call | solution.py:426
  (75 shorter events, 15.0 us)
Async XLA Ops:
  3.9 12.1 %collective-permute-start = (bf16[160,1152]{1,0:T(8,128)(2,1)}, bf16[160,1152]{1,0:T(8,128)(2,1)S(1)}, u32[]{:S(2)}, u32[]{:S(2)}) collective-permute-start(bf16[160,1152]{1,0:T(8,128)(2,1)} %ends.1), channel_id=1, source_target_pairs={{0,4},{1,5},{4,0},{5,1},{8,12},{9,13},{12,8},{13,9},{2,6},{3,7},{6... | collective-permute-start | bytes 1105928 | tf_op jit(solution)/shard_map/ppermute | solution.py:595
  14.1 10.2 %collective-permute-start.1 = (bf16[160,1152]{1,0:T(8,128)(2,1)S(1)}, bf16[160,1152]{1,0:T(8,128)(2,1)S(1)}, u32[]{:S(2)}, u32[]{:S(2)}) collective-permute-start(bf16[160,1152]{1,0:T(8,128)(2,1)S(1)} %get-tuple-element.54), channel_id=1, source_target_pairs={{0,4},{1,5},{4,0},{5,1},{8,12},{9,13},{12,8},{13,9},{2,6},{3,7},{6... | collective-permute-start | bytes 1105928 | tf_op jit(solution)/shard_map/ppermute | solution.py:595
  16.3 14.2 %collective-permute-start.2 = (bf16[160,1152]{1,0:T(8,128)(2,1)S(1)}, bf16[160,1152]{1,0:T(8,128)(2,1)S(1)}, u32[]{:S(2)}, u32[]{:S(2)}) collective-permute-start(bf16[160,1152]{1,0:T(8,128)(2,1)S(1)} %get-tuple-element.56), channel_id=1, source_target_pairs={{0,1},{1,0},{4,8},{5,9},{8,4},{9,5},{12,13},{13,12},{2,3},{3,2},{6... | collective-permute-start | bytes 1105928 | tf_op jit(solution)/shard_map/ppermute | solution.py:595
  22.7 11.2 %collective-permute-start.3 = (bf16[160,1152]{1,0:T(8,128)(2,1)S(1)}, bf16[160,1152]{1,0:T(8,128)(2,1)S(1)}, u32[]{:S(2)}, u32[]{:S(2)}) collective-permute-start(bf16[160,1152]{1,0:T(8,128)(2,1)S(1)} %get-tuple-element.59), channel_id=1, source_target_pairs={{0,2},{2,0},{1,3},{3,1},{4,6},{6,4},{5,7},{7,5},{8,10},{10,8},{9,1... | collective-permute-start | bytes 1105928 | tf_op jit(solution)/shard_map/ppermute | solution.py:499
  24.5 9.7 %collective-permute-start.4 = (bf16[160,1152]{1,0:T(8,128)(2,1)S(1)}, bf16[160,1152]{1,0:T(8,128)(2,1)S(1)}, u32[]{:S(2)}, u32[]{:S(2)}) collective-permute-start(bf16[160,1152]{1,0:T(8,128)(2,1)S(1)} %get-tuple-element.62), channel_id=1, source_target_pairs={{0,1},{1,0},{4,8},{5,9},{8,4},{9,5},{12,13},{13,12},{2,3},{3,2},{6... | collective-permute-start | bytes 1105928 | tf_op jit(solution)/shard_map/ppermute | solution.py:595
  29.0 14.7 %collective-permute-start.6 = (bf16[160,1152]{1,0:T(8,128)(2,1)S(1)}, bf16[160,1152]{1,0:T(8,128)(2,1)S(1)}, u32[]{:S(2)}, u32[]{:S(2)}) collective-permute-start(bf16[160,1152]{1,0:T(8,128)(2,1)S(1)} %get-tuple-element.66), channel_id=1, source_target_pairs={{0,2},{2,0},{1,3},{3,1},{4,6},{6,4},{5,7},{7,5},{8,10},{10,8},{9,1... | collective-permute-start | bytes 1105928 | tf_op jit(solution)/shard_map/ppermute | solution.py:499
  30.7 12.6 %collective-permute-start.5 = (bf16[160,1152]{1,0:T(8,128)(2,1)S(1)}, bf16[160,1152]{1,0:T(8,128)(2,1)S(1)}, u32[]{:S(2)}, u32[]{:S(2)}) collective-permute-start(bf16[160,1152]{1,0:T(8,128)(2,1)S(1)} %get-tuple-element.64), channel_id=1, source_target_pairs={{0,4},{1,5},{4,0},{5,1},{8,12},{9,13},{12,8},{13,9},{2,6},{3,7},{6... | collective-permute-start | bytes 1105928 | tf_op jit(solution)/shard_map/ppermute | solution.py:595
  34.2 9.7 %collective-permute-start.7 = (bf16[160,1152]{1,0:T(8,128)(2,1)S(1)}, bf16[160,1152]{1,0:T(8,128)(2,1)S(1)}, u32[]{:S(2)}, u32[]{:S(2)}) collective-permute-start(bf16[160,1152]{1,0:T(8,128)(2,1)S(1)} %get-tuple-element.67), channel_id=1, source_target_pairs={{0,1},{1,0},{4,8},{5,9},{8,4},{9,5},{12,13},{13,12},{2,3},{3,2},{6... | collective-permute-start | bytes 1105928 | tf_op jit(solution)/shard_map/ppermute | solution.py:595
  34.5 16.8 %collective-permute-start.8 = (bf16[160,1152]{1,0:T(8,128)(2,1)S(1)}, bf16[160,1152]{1,0:T(8,128)(2,1)S(1)}, u32[]{:S(2)}, u32[]{:S(2)}) collective-permute-start(bf16[160,1152]{1,0:T(8,128)(2,1)S(1)} %get-tuple-element.69), channel_id=1, source_target_pairs={{0,4},{1,5},{4,0},{5,1},{8,12},{9,13},{12,8},{13,9},{2,6},{3,7},{6... | collective-permute-start | bytes 1105928 | tf_op jit(solution)/shard_map/ppermute | solution.py:595
  43.6 9.6 %collective-permute-start.9 = (bf16[160,1152]{1,0:T(8,128)(2,1)S(1)}, bf16[160,1152]{1,0:T(8,128)(2,1)S(1)}, u32[]{:S(2)}, u32[]{:S(2)}) collective-permute-start(bf16[160,1152]{1,0:T(8,128)(2,1)S(1)} %get-tuple-element.72), channel_id=1, source_target_pairs={{0,1},{1,0},{4,8},{5,9},{8,4},{9,5},{12,13},{13,12},{2,3},{3,2},{6... | collective-permute-start | bytes 1105928 | tf_op jit(solution)/shard_map/ppermute | solution.py:595
  44.0 14.1 %collective-permute-start.10 = (bf16[160,1152]{1,0:T(8,128)(2,1)S(1)}, bf16[160,1152]{1,0:T(8,128)(2,1)S(1)}, u32[]{:S(2)}, u32[]{:S(2)}) collective-permute-start(bf16[160,1152]{1,0:T(8,128)(2,1)S(1)} %get-tuple-element.74), channel_id=1, source_target_pairs={{0,4},{1,5},{4,0},{5,1},{8,12},{9,13},{12,8},{13,9},{2,6},{3,7},{6... | collective-permute-start | bytes 1105928 | tf_op jit(solution)/shard_map/ppermute | solution.py:595
  51.6 7.6 %collective-permute-start.15 = (bf16[160,1152]{1,0:T(8,128)(2,1)S(1)}, bf16[160,1152]{1,0:T(8,128)(2,1)S(1)}, u32[]{:S(2)}, u32[]{:S(2)}) collective-permute-start(bf16[160,1152]{1,0:T(8,128)(2,1)S(1)} %get-tuple-element.83.refs_0_), channel_id=1, source_target_pairs={{0,2},{2,0},{1,3},{3,1},{4,6},{6,4},{5,7},{7,5},{8,10},{10,8},{9,1... | collective-permute-start | bytes 1105928 | tf_op jit(solution)/shard_map/ppermute | solution.py:544
  53.4 12.6 %collective-permute-start.12 = (bf16[160,1152]{1,0:T(8,128)(2,1)S(1)}, bf16[160,1152]{1,0:T(8,128)(2,1)S(1)}, u32[]{:S(2)}, u32[]{:S(2)}) collective-permute-start(bf16[160,1152]{1,0:T(8,128)(2,1)S(1)} %get-tuple-element.78), channel_id=1, source_target_pairs={{0,4},{1,5},{4,0},{5,1},{8,12},{9,13},{12,8},{13,9},{2,6},{3,7},{6... | collective-permute-start | bytes 1105928 | tf_op jit(solution)/shard_map/ppermute | solution.py:595
  58.3 8.0 %collective-permute-start.13 = (bf16[160,1152]{1,0:T(8,128)(2,1)S(1)}, bf16[160,1152]{1,0:T(8,128)(2,1)S(1)}, u32[]{:S(2)}, u32[]{:S(2)}) collective-permute-start(bf16[160,1152]{1,0:T(8,128)(2,1)S(1)} %get-tuple-element.80), channel_id=1, source_target_pairs={{0,1},{1,0},{4,8},{5,9},{8,4},{9,5},{12,13},{13,12},{2,3},{3,2},{6... | collective-permute-start | bytes 1105928 | tf_op jit(solution)/shard_map/ppermute | solution.py:595
  58.4 15.3 %collective-permute-start.16 = (bf16[160,1152]{1,0:T(8,128)(2,1)S(1)}, bf16[160,1152]{1,0:T(8,128)(2,1)S(1)}, u32[]{:S(2)}, u32[]{:S(2)}) collective-permute-start(bf16[160,1152]{1,0:T(8,128)(2,1)S(1)} %get-tuple-element.83.refs_0_), channel_id=1, source_target_pairs={{0,1},{1,0},{2,3},{3,2},{4,5},{5,4},{6,7},{7,6},{8,9},{9,8},{10,11... | collective-permute-start | bytes 1105928 | tf_op jit(solution)/shard_map/ppermute | solution.py:547
  59.2 14.5 %collective-permute-start.17 = (bf16[160,1152]{1,0:T(8,128)(2,1)S(1)}, bf16[160,1152]{1,0:T(8,128)(2,1)S(1)}, u32[]{:S(2)}, u32[]{:S(2)}) collective-permute-start(bf16[160,1152]{1,0:T(8,128)(2,1)S(1)} %collective-permute-done.15.refs_1_), channel_id=1, source_target_pairs={{0,1},{1,0},{2,3},{3,2},{4,5},{5,4},{6,7},{7,6},{8,9},{9,8},{10,11... | collective-permute-start | bytes 1105928 | tf_op jit(solution)/shard_map/ppermute | solution.py:547
  59.3 19.0 %collective-permute-start.14 = (bf16[160,1152]{1,0:T(8,128)(2,1)S(1)}, bf16[160,1152]{1,0:T(8,128)(2,1)S(1)}, u32[]{:S(2)}, u32[]{:S(2)}) collective-permute-start(bf16[160,1152]{1,0:T(8,128)(2,1)S(1)} %get-tuple-element.82), channel_id=1, source_target_pairs={{0,4},{1,5},{4,0},{5,1},{8,12},{9,13},{12,8},{13,9},{2,6},{3,7},{6... | collective-permute-start | bytes 1105928 | tf_op jit(solution)/shard_map/ppermute | solution.py:595
  66.2 12.2 %collective-permute-start.18 = (bf16[160,1152]{1,0:T(8,128)(2,1)S(1)}, bf16[160,1152]{1,0:T(8,128)(2,1)S(1)}, u32[]{:S(2)}, u32[]{:S(2)}) collective-permute-start(bf16[160,1152]{1,0:T(8,128)(2,1)S(1)} %get-tuple-element.86), channel_id=1, source_target_pairs={{0,1},{1,0},{4,8},{5,9},{8,4},{9,5},{12,13},{13,12},{2,3},{3,2},{6... | collective-permute-start | bytes 1105928 | tf_op jit(solution)/shard_map/ppermute | solution.py:595
  66.6 14.4 %collective-permute-start.19 = (bf16[160,1152]{1,0:T(8,128)(2,1)S(1)}, bf16[160,1152]{1,0:T(8,128)(2,1)S(1)}, u32[]{:S(2)}, u32[]{:S(2)}) collective-permute-start(bf16[160,1152]{1,0:T(8,128)(2,1)S(1)} %get-tuple-element.88), channel_id=1, source_target_pairs={{0,4},{1,5},{4,0},{5,1},{8,12},{9,13},{12,8},{13,9},{2,6},{3,7},{6... | collective-permute-start | bytes 1105928 | tf_op jit(solution)/shard_map/ppermute | solution.py:595
  81.3 8.6 %collective-permute-start.23 = (bf16[160,1152]{1,0:T(8,128)(2,1)S(1)}, bf16[160,1152]{1,0:T(8,128)(2,1)S(1)}, u32[]{:S(2)}, u32[]{:S(2)}) collective-permute-start(bf16[160,1152]{1,0:T(8,128)(2,1)S(1)} %get-tuple-element.94.refs_0_), channel_id=1, source_target_pairs={{0,2},{2,0},{1,3},{3,1},{4,6},{6,4},{5,7},{7,5},{8,10},{10,8},{9,1... | collective-permute-start | bytes 1105928 | tf_op jit(solution)/shard_map/ppermute | solution.py:544
  82.0 7.8 %collective-permute-start.20 = (bf16[160,1152]{1,0:T(8,128)(2,1)S(1)}, bf16[160,1152]{1,0:T(8,128)(2,1)S(1)}, u32[]{:S(2)}, u32[]{:S(2)}) collective-permute-start(bf16[160,1152]{1,0:T(8,128)(2,1)S(1)} %get-tuple-element.90), channel_id=1, source_target_pairs={{0,1},{1,0},{4,8},{5,9},{8,4},{9,5},{12,13},{13,12},{2,3},{3,2},{6... | collective-permute-start | bytes 1105928 | tf_op jit(solution)/shard_map/ppermute | solution.py:595
  82.0 11.0 %collective-permute-start.21 = (bf16[160,1152]{1,0:T(8,128)(2,1)S(1)}, bf16[160,1152]{1,0:T(8,128)(2,1)S(1)}, u32[]{:S(2)}, u32[]{:S(2)}) collective-permute-start(bf16[160,1152]{1,0:T(8,128)(2,1)S(1)} %get-tuple-element.92), channel_id=1, source_target_pairs={{0,4},{1,5},{4,0},{5,1},{8,12},{9,13},{12,8},{13,9},{2,6},{3,7},{6... | collective-permute-start | bytes 1105928 | tf_op jit(solution)/shard_map/ppermute | solution.py:595
  84.5 12.2 %collective-permute-start.24 = (bf16[160,1152]{1,0:T(8,128)(2,1)S(1)}, bf16[160,1152]{1,0:T(8,128)(2,1)S(1)}, u32[]{:S(2)}, u32[]{:S(2)}) collective-permute-start(bf16[160,1152]{1,0:T(8,128)(2,1)S(1)} %get-tuple-element.94.refs_0_), channel_id=1, source_target_pairs={{0,1},{1,0},{2,3},{3,2},{4,5},{5,4},{6,7},{7,6},{8,9},{9,8},{10,11... | collective-permute-start | bytes 1105928 | tf_op jit(solution)/shard_map/ppermute | solution.py:547
  90.0 11.3 %collective-permute-start.22 = (bf16[160,1152]{1,0:T(8,128)(2,1)S(1)}, bf16[160,1152]{1,0:T(8,128)(2,1)S(1)}, u32[]{:S(2)}, u32[]{:S(2)}) collective-permute-start(bf16[160,1152]{1,0:T(8,128)(2,1)S(1)} %get-tuple-element.93), channel_id=1, source_target_pairs={{0,4},{1,5},{4,0},{5,1},{8,12},{9,13},{12,8},{13,9},{2,6},{3,7},{6... | collective-permute-start | bytes 1105928 | tf_op jit(solution)/shard_map/ppermute | solution.py:595
  (9 other events, 33.8 us)

commit v2 on v1

--- a/solution.py
+++ b/solution.py
@@ -9,7 +9,7 @@
 from jax.sharding import PartitionSpec as P
 
 
-LAG = 3
+LAG, TAKEN_BY = 3, 4
 SPLIT = ()
 SKIPPED = (4,)
 SUMS_FIRST, SUMS_CHUNK, ROWS_CHUNK, OWN_WEIGHT = 3, 1, 0, -0.7
@@ -92,7 +92,7 @@
     return table_ref[kind_ref[system], expert]
 
 
-def merge_kernel(expert_size, sys_size, first, tile, table_ref, kind_ref, weights_ref, *out_refs):
+def merge_kernel(expert_size, sys_size, first, table_ref, kind_ref, weights_ref, *out_refs):
     experts, _, width = weights_ref.shape
     rows = out_refs[0].shape[0]
     place = lax.axis_index("expert")
@@ -105,36 +105,35 @@
         for k in range(expert_size)
     ]
 
-    def step(block_ref, *parts):
-        for start in range(0, tile, 16):
-            span = pl.ds(start, 16)
+    lanes = 384 if width % 384 == 0 else width
+
+    def step(i, _):
+        for lane in range(0, width, lanes):
+            columns = pl.ds(lane, lanes)
+            here = pl.ds(pl.multiple_of(first + i * 16, 16), 16)
             totals = [None] * expert_size
             for e in range(experts):
-                weight = block_ref[e, span, :].astype(jnp.float32)
+                weight = weights_ref[e, here, columns].astype(jnp.float32)
                 for k in range(expert_size):
                     term = factors[k][e] * weight
                     totals[k] = term if totals[k] is None else totals[k] + term
             for k in range(expert_size):
-                parts[k][span, :] = totals[k].astype(jnp.bfloat16)
-
-    pltpu.emit_pipeline(
-        step,
-        grid=(rows // tile,),
-        in_specs=[pl.BlockSpec((experts, tile, width), lambda i: (0, first // tile + i, 0))],
-        out_specs=[pl.BlockSpec((tile, width), lambda i: (i, 0))] * expert_size,
-    )(weights_ref, *out_refs)
-
-
-def merge_part(table, kind, weights, expert_size, sys_size, first, rows, tile):
+                out_refs[k][pl.ds(pl.multiple_of(i * 16, 16), 16), columns] = totals[k].astype(jnp.bfloat16)
+        return 0
+
+    lax.fori_loop(0, rows // 16, step, 0)
+
+
+def merge_part(table, kind, weights, expert_size, sys_size, first, rows):
     experts, _, width = weights.shape
     return pl.pallas_call(
-        functools.partial(merge_kernel, expert_size, sys_size, first, tile),
+        functools.partial(merge_kernel, expert_size, sys_size, first),
         in_specs=[
             pl.BlockSpec(memory_space=pltpu.SMEM),
             pl.BlockSpec(memory_space=pltpu.SMEM),
-            pl.BlockSpec(memory_space=pltpu.HBM),
-        ],
-        out_specs=[pl.BlockSpec(memory_space=pl.ANY)] * expert_size,
+            pl.BlockSpec(memory_space=pltpu.VMEM),
+        ],
+        out_specs=[pl.BlockSpec(memory_space=pltpu.VMEM)] * expert_size,
         out_shape=[jax.ShapeDtypeStruct((rows, width), jnp.bfloat16)] * expert_size,
         compiler_params=pltpu.CompilerParams(vmem_limit_bytes=8 << 20),
         cost_estimate=pl.CostEstimate(
@@ -247,66 +246,44 @@
     )(counts, features, grad)
 
 
-def input_kernel(live_ref, rows_ref, out_ref):
-    out_ref[...] = lax.dot_general(
-        live_ref[...], rows_ref[...], (((1,), (1,)), ((), ())), preferred_element_type=jnp.float32
-    ).astype(out_ref.dtype)
-
-
-def input_product(live, store, width_in):
+def columns_kernel(width_in, firsts, live_ref, store_ref, *refs):
+    out_ref, token_ref, part, done = refs[-4:]
+    token_ref[...] = jnp.zeros_like(token_ref)
+    count, _, tile = part.shape
+    first = at_device(firsts)
+    writes = []
+    for t in range(count):
+        columns = pl.ds(pl.multiple_of(first + t * tile, 128), tile)
+        rows = pl.ds(pl.multiple_of(width_in + first + t * tile, 16), tile)
+        part[t] = lax.dot_general(
+            live_ref[...], store_ref[rows, :], (((1,), (1,)), ((), ())), preferred_element_type=jnp.float32
+        ).astype(part.dtype)
+        writes.append(pltpu.make_async_copy(part.at[t], out_ref.at[:, columns], done.at[t]))
+        writes[-1].start()
+    for write in writes:
+        write.wait()
+
+
+def columns(live, store, product, width_in, firsts, count, tile):
     edges, width = live.shape
-    tile = 256 if width_in % 256 == 0 else width_in
+    vmem = pl.BlockSpec(memory_space=pltpu.VMEM)
+    keep = pl.BlockSpec(memory_space=pl.ANY)
     return pl.pallas_call(
-        input_kernel,
-        grid=(width_in // tile,),
-        in_specs=[
-            pl.BlockSpec((edges, width), lambda i: (0, 0)),
-            pl.BlockSpec((tile, width), lambda i: (width_in // tile + i, 0)),
-        ],
-        out_specs=pl.BlockSpec((edges, tile), lambda i: (0, i)),
-        out_shape=jax.ShapeDtypeStruct((edges, width_in), jnp.bfloat16),
-        compiler_params=pltpu.CompilerParams(vmem_limit_bytes=12 << 20),
+        functools.partial(columns_kernel, width_in, firsts),
+        in_specs=[vmem, vmem] + ([] if product is None else [keep]),
+        out_specs=[keep, vmem],
+        out_shape=[
+            jax.ShapeDtypeStruct((edges, width_in), jnp.bfloat16),
+            jax.ShapeDtypeStruct((8, 128), jnp.float32),
+        ],
+        input_output_aliases={} if product is None else {2: 0},
+        scratch_shapes=[pltpu.VMEM((count, edges, tile), jnp.bfloat16), pltpu.SemaphoreType.DMA((count,))],
+        compiler_params=pltpu.CompilerParams(vmem_limit_bytes=8 << 20),
         cost_estimate=pl.CostEstimate(
-            flops=2 * edges * width_in * width,
-            bytes_accessed=2 * (edges * width_in + edges * width + width_in * width),
-            transcendentals=0,
+            flops=2 * edges * count * tile * width, bytes_accessed=2 * edges * count * tile, transcendentals=0
         ),
-        name="input_product",
-    )(live, store)
-
-
-def last_kernel(width_in, windows, live_ref, store_ref, _, out_ref, part, done):
-    lanes = part.shape[1]
-    first = pl.multiple_of(at_device(windows), 128)
-    part[...] = lax.dot_general(
-        live_ref[...],
-        store_ref[pl.ds(pl.multiple_of(width_in + first, 128), lanes), :],
-        (((1,), (1,)), ((), ())),
-        preferred_element_type=jnp.float32,
-    ).astype(part.dtype)
-    write = pltpu.make_async_copy(part, out_ref.at[:, pl.ds(first, lanes)], done)
-    write.start()
-    write.wait()
-
-
-def last_product(live, store, product, rows, places):
-    edges, width_in = product.shape
-    lanes = min(width_in, max(-(-(place * rows % 128 + rows) // 128) * 128 for place in places))
-    windows = [min(place * rows // 128 * 128, width_in - lanes) for place in places]
-    vmem = pl.BlockSpec(memory_space=pltpu.VMEM)
-    return pl.pallas_call(
-        functools.partial(last_kernel, width_in, windows),
-        in_specs=[vmem, vmem, pl.BlockSpec(memory_space=pl.ANY)],
-        out_specs=pl.BlockSpec(memory_space=pl.ANY),
-        out_shape=jax.ShapeDtypeStruct(product.shape, product.dtype),
-        input_output_aliases={2: 0},
-        scratch_shapes=[pltpu.VMEM((edges, lanes), jnp.bfloat16), pltpu.SemaphoreType.DMA],
-        compiler_params=pltpu.CompilerParams(vmem_limit_bytes=4 << 20),
-        cost_estimate=pl.CostEstimate(
-            flops=2 * edges * lanes * live.shape[1], bytes_accessed=2 * edges * lanes, transcendentals=0
-        ),
-        name="last_product",
-    )(live, store, product)
+        name="columns",
+    )(live, store, *([] if product is None else [product]))
 
 
 def hop_kernel(count, behind, take, add, origin, *refs):
@@ -492,9 +469,7 @@
     store, live = outer_products(edge_counts, features, grad, sys_size, (2 * places + 1) * rows)
     exchanged = []
     for h in range(chunks):
-        parts = merge_part(
-            coef_table, system_kind, expert_weights, expert_size, sys_size, h * rows, rows, tile
-        )
+        parts = merge_part(coef_table, system_kind, expert_weights, expert_size, sys_size, h * rows, rows)
         arrays = [parts[0]]
         arrays += [lax.ppermute(parts[k], "expert", shift(expert_size, k)) for k in range(1, expert_size)]
         exchanged.append(arrays)
@@ -549,19 +524,25 @@
             tokens[h] = token
         return store, result
 
-    used = [at for at, step in enumerate(steps) if step]
-    last, first_of_last = {}, used[-1]
-    for at in reversed(used[-2:]):
-        new = {target: b * chunks + h for _, target, kind, b, h, _ in steps[at] if kind == "M"}
-        if set(new) & set(last):
-            break
-        last.update(new)
-        first_of_last = at
-    product = None
-
-    def whole_product(store):
-        return input_product(live, store, width_in)
-
+    def early_columns(settled):
+        tiles, firsts = width_in // wide, []
+        for z in range(edge_size):
+            missing = [
+                extent(h, part)[0] + b * row_count + r
+                for at, part in moves
+                if (at, part) not in settled
+                for _, target, kind, b, h, _ in steps[at]
+                if (target, kind) == (z, "M")
+                for r in (0, extent(h, part)[1] - 1)
+            ]
+            low, high = min(missing, default=width_in), max(missing, default=0) + 1
+            before, after = low // wide, (width_in - high) // wide
+            tiles = min(tiles, max(before, after))
+            firsts.append(before >= after)
+        return tiles, [0 if first else width_in - tiles * wide for first in firsts]
+
+    wide = 256 if width_in % 256 == 0 else width_in
+    product, tiles, firsts_early = None, 0, [0] * edge_size
     for move in moves:
         at, part = move
         step = steps[at]
@@ -577,12 +558,14 @@
             if came is not None:
                 brought = parts_of(came, halves)
                 needed |= {(came, one) for one in brought if part is None or one is None or one == part}
-        due = [one for one in pending if one in needed or one[0] <= at - LAG]
+        due = [one for one in pending if one in needed or one[0] <= at - TAKEN_BY]
         for one in due:
-            waits = one[0] >= first_of_last
-            if waits and product is None:
-                product = whole_product(store)
-            behind = overdue(at) + ([product] if waits else [])
+            behind = overdue(at)
+            if move == moves[-1] and one == due[-1]:
+                tiles, firsts_early = early_columns([each for each in moves[:-1] if each not in pending])
+                if tiles:
+                    product, token = columns(live, store, None, width_in, firsts_early, tiles, wide)
+                    behind.append(token)
             if one == due[-1]:
                 store, message = settle(store, one, origin, count, behind)
             else:
@@ -596,15 +579,13 @@
         pending.append(move)
         store, result = finish(store, result)
     while pending:
-        waits = pending[0][0] >= first_of_last
-        if waits and product is None:
-            product = whole_product(store)
-        behind = (list(tokens.values()) if len(pending) == 1 else []) + ([product] if waits else [])
-        (store,) = settle(store, pending[0], None, rows, behind)
+        (store,) = settle(store, pending[0], None, rows, list(tokens.values()) if len(pending) == 1 else ())
         store, result = finish(store, result)
-    last = [last.get(z, 0) for z in range(edge_size)]
-    input_grad = last_product(live, store, product, rows, last)
-    return (input_grad[None], result)
+    rest = width_in // wide - tiles
+    if rest:
+        firsts_late = [0 if first else tiles * wide for first in firsts_early]
+        product, _ = columns(live, store, product, width_in, firsts_late, rest, wide)
+    return (product[None], result)
 
 
 def solution(mesh):

time: 103 us -> 103 us (level)
  waiting for transfers between devices: 24.6 us -> 37.7 us
  starting transfers between devices: 37.2 us -> 27.5 us
  Pallas kernels: 34.6 us -> 31.6 us
    ppermute x18, starting transfers between devices: 32.2 us -> 21.7 us  [body(): lax.ppermute(message, ('edge', 'sys'), swaps(at, edge_size, sys_size))]
    ppermute x18, waiting for transfers between devices: 19 us -> 27.1 us  [body(): lax.ppermute(message, ('edge', 'sys'), swaps(at, edge_size, sys_size))]
    ppermute x2, waiting for transfers between devices: 0.01 us -> 3.8 us  [body(): lax.ppermute(parts[k], 'expert', shift(expert_size, k))]
    pallas_call x2, Pallas kernels: 8.73 us -> 6.5 us  [merge_part(): pl.pallas_call(functools.partial(merge_kernel, expert_size, sys_size, fir...]
    ppermute x2, starting transfers between devices: 1.39 us -> 2.63 us  [finish(): column.append(lax.ppermute(rows_h, 'expert', shift(expert_size, k)))]
    ppermute x2, waiting for transfers between devices: 5.65 us -> 6.74 us  [finish(): column.append(lax.ppermute(rows_h, 'expert', shift(expert_size, k)))]
    pallas_call x24 -> x28, Pallas kernels: 3.9 us -> 3.91 us  [hop(): pl.pallas_call(functools.partial(hop_kernel, len(arrays), len(behind), ta...]
    unnamed x14 -> x12, local copies, waits for them, and re-layouts: 5.15 us -> 5.15 us
  transfers between devices with their start and end apart: 26 -> 26, of which waited for: 9 -> 12; matrix products, arithmetic and copies ran while one was open for 0% -> 0% of each run, Pallas kernels for 29% -> 25%
where the time goes in v2:
time: 103 us
  waiting for transfers between devices  37.7 us (37%)
  Pallas kernels  31.6 us (31%)
  starting transfers between devices  27.5 us (27%)
  local copies, waits for them, and re-layouts  5.15 us (5%)
  between operations  1.03 us (1%)
    ppermute x18, waiting for transfers between devices, body(): lax.ppermute(message, ('edge', 'sys'), swaps(at, edge_size, sys_size))  27.1 us
    ppermute x18, starting transfers between devices, body(): lax.ppermute(message, ('edge', 'sys'), swaps(at, edge_size, sys_size))  21.7 us
    pallas_call x2, Pallas kernels, spread(): pl.pallas_call(functools.partial(spread_kernel, count, groups), grid=(row...  9.21 us
    ppermute x2, waiting for transfers between devices, finish(): column.append(lax.ppermute(rows_h, 'expert', shift(expert_size, k)))  6.74 us
    pallas_call x2, Pallas kernels, merge_part(): pl.pallas_call(functools.partial(merge_kernel, expert_size, sys_size, fir...  6.5 us
    unnamed x12, local copies, waits for them, and re-layouts  5.15 us
    pallas_call x2, Pallas kernels, columns(): pl.pallas_call(functools.partial(columns_kernel, width_in, firsts), in_sp...  4 us
    pallas_call x28, Pallas kernels, hop(): pl.pallas_call(functools.partial(hop_kernel, len(arrays), len(behind), ta...  3.91 us
  transfers between devices with their start and end apart: 26, of which 12 were waited for; matrix products, arithmetic and copies ran while one was open for 0% of the time, Pallas kernels for 25%

profile of v2, /device:TPU:0, one launch (start us, length us, event | category | flops | bytes accessed | tf_op | source)
XLA Modules:
  0.0 102.9 jit_solution(14393088251742164092)
XLA Ops:
  0.6 3.3 %ends.1 = bf16[160,1152]{1,0:T(8,128)(2,1)} custom-call(s32[4]{0:T(128)} %counts_ref.3, bf16[448,1280]{1,0:T(8,128)(2,1)} %bitcast.3, bf16[448,1152]{1,0:T(8,128)(2,1)} %bitcast.5), custom_call_target="tpu_custom_call" | custom-call | flops 264241152 | bytes 1261568 | tf_op jit(solution)/shard_map/ends/pallas_call | solution.py:186
  3.9 3.1 %collective-permute-start = (bf16[160,1152]{1,0:T(8,128)(2,1)}, bf16[160,1152]{1,0:T(8,128)(2,1)S(1)}, u32[]{:S(2)}, u32[]{:S(2)}) collective-permute-start(bf16[160,1152]{1,0:T(8,128)(2,1)} %ends.1), channel_id=1, source_target_pairs={{0,4},{1,5},{4,0},{5,1},{8,12},{9,13},{12,8},{13,9},{2,6},{3,7},{6... | collective-permute-start | bytes 1105928 | tf_op jit(solution)/shard_map/ppermute | solution.py:578
  10.1 3.9 %outer.1 = (bf16[2720,1152]{1,0:T(8,128)(2,1)S(1)}, bf16[448,1152]{1,0:T(8,128)(2,1)S(1)}) custom-call(s32[4]{0:T(128)S(1)} %copy-done.5, bf16[448,1280]{1,0:T(8,128)(2,1)S(1)} %bitcast.4, bf16[448,1152]{1,0:T(8,128)(2,1)S(1)} %bitcast.6), custom_call_target="tpu_custom_call" | custom-call | flops 1321205760 | bytes 5128192 | tf_op jit(solution)/shard_map/outer/pallas_call | solution.py:223
  14.2 1.8 %collective-permute-done.refs_1_ = bf16[160,1152]{1,0:T(8,128)(2,1)S(1)} collective-permute-done((bf16[160,1152]{1,0:T(8,128)(2,1)}, bf16[160,1152]{1,0:T(8,128)(2,1)S(1)}, u32[]{:S(2)}, u32[]{:S(2)}) %collective-permute-start) | collective-permute-done | bytes 368672 | tf_op jit(solution)/shard_map/ppermute | solution.py:578
  16.4 2.0 %copy-done = bf16[16,320,1152]{2,1,0:T(8,128)(2,1)S(1)} copy-done((bf16[16,320,1152]{2,1,0:T(8,128)(2,1)S(1)}, bf16[16,320,1152]{2,1,0:T(8,128)(2,1)}, u32[]{:S(2)}) %copy-start) | copy-done | bytes 11796504
  18.4 3.3 %merge.2 = (bf16[160,1152]{1,0:T(8,128)(2,1)S(1)}, bf16[160,1152]{1,0:T(8,128)(2,1)S(1)}) custom-call(f32[16,32]{1,0:T(8,128)S(1)} %copy-done.3, s32[4]{0:T(128)S(1)} %copy-done.4, bf16[16,320,1152]{2,1,0:T(8,128)(2,1)S(1)} %copy-done), custom_call_target="tpu_custom_call" | custom-call | flops 11796480 | bytes 5898240 | tf_op jit(solution)/shard_map/merge/pallas_call | solution.py:129
  24.8 3.2 %collective-permute-start.5 = (bf16[160,1152]{1,0:T(8,128)(2,1)S(1)}, bf16[160,1152]{1,0:T(8,128)(2,1)S(1)}, u32[]{:S(2)}, u32[]{:S(2)}) collective-permute-start(bf16[160,1152]{1,0:T(8,128)(2,1)S(1)} %get-tuple-element.67), channel_id=1, source_target_pairs={{0,4},{1,5},{4,0},{5,1},{8,12},{9,13},{12,8},{13,9},{2,6},{3,7},{6... | collective-permute-start | bytes 1105928 | tf_op jit(solution)/shard_map/ppermute | solution.py:578
  28.0 3.2 %merge.3 = (bf16[160,1152]{1,0:T(8,128)(2,1)S(1)}, bf16[160,1152]{1,0:T(8,128)(2,1)S(1)}) custom-call(f32[16,32]{1,0:T(8,128)S(1)} %copy-done.3, s32[4]{0:T(128)S(1)} %copy-done.4, bf16[16,320,1152]{2,1,0:T(8,128)(2,1)S(1)} %copy-done), custom_call_target="tpu_custom_call" | custom-call | flops 11796480 | bytes 5898240 | tf_op jit(solution)/shard_map/merge/pallas_call | solution.py:129
  33.2 2.1 %collective-permute-start.8 = (bf16[160,1152]{1,0:T(8,128)(2,1)S(1)}, bf16[160,1152]{1,0:T(8,128)(2,1)S(1)}, u32[]{:S(2)}, u32[]{:S(2)}) collective-permute-start(bf16[160,1152]{1,0:T(8,128)(2,1)S(1)} %get-tuple-element.73), channel_id=1, source_target_pairs={{0,4},{1,5},{4,0},{5,1},{8,12},{9,13},{12,8},{13,9},{2,6},{3,7},{6... | collective-permute-start | bytes 1105928 | tf_op jit(solution)/shard_map/ppermute | solution.py:578
  36.2 3.8 %collective-permute-done.6.refs_2_ = bf16[160,1152]{1,0:T(8,128)(2,1)S(1)} collective-permute-done((bf16[160,1152]{1,0:T(8,128)(2,1)S(1)}, bf16[160,1152]{1,0:T(8,128)(2,1)S(1)}, u32[]{:S(2)}, u32[]{:S(2)}) %collective-permute-start.6) | collective-permute-done | bytes 368672 | tf_op jit(solution)/shard_map/ppermute | solution.py:474
  41.2 3.1 %collective-permute-done.8.refs_1_ = bf16[160,1152]{1,0:T(8,128)(2,1)S(1)} collective-permute-done((bf16[160,1152]{1,0:T(8,128)(2,1)S(1)}, bf16[160,1152]{1,0:T(8,128)(2,1)S(1)}, u32[]{:S(2)}, u32[]{:S(2)}) %collective-permute-start.8) | collective-permute-done | bytes 368672 | tf_op jit(solution)/shard_map/ppermute | solution.py:578
  46.9 5.9 %collective-permute-start.12 = (bf16[160,1152]{1,0:T(8,128)(2,1)S(1)}, bf16[160,1152]{1,0:T(8,128)(2,1)S(1)}, u32[]{:S(2)}, u32[]{:S(2)}) collective-permute-start(bf16[160,1152]{1,0:T(8,128)(2,1)S(1)} %get-tuple-element.81), channel_id=1, source_target_pairs={{0,4},{1,5},{4,0},{5,1},{8,12},{9,13},{12,8},{13,9},{2,6},{3,7},{6... | collective-permute-start | bytes 1105928 | tf_op jit(solution)/shard_map/ppermute | solution.py:578
  52.8 1.9 %collective-permute-done.14.refs_1_ = bf16[160,1152]{1,0:T(8,128)(2,1)S(1)} collective-permute-done((bf16[160,1152]{1,0:T(8,128)(2,1)S(1)}, bf16[160,1152]{1,0:T(8,128)(2,1)S(1)}, u32[]{:S(2)}, u32[]{:S(2)}) %collective-permute-start.14) | collective-permute-done | bytes 368672 | tf_op jit(solution)/shard_map/ppermute | solution.py:519
  54.7 2.4 %collective-permute-done.10.refs_1_ = bf16[160,1152]{1,0:T(8,128)(2,1)S(1)} collective-permute-done((bf16[160,1152]{1,0:T(8,128)(2,1)S(1)}, bf16[160,1152]{1,0:T(8,128)(2,1)S(1)}, u32[]{:S(2)}, u32[]{:S(2)}) %collective-permute-start.10) | collective-permute-done | bytes 368672 | tf_op jit(solution)/shard_map/ppermute | solution.py:578
  57.9 7.1 %collective-permute-done.12.refs_1_ = bf16[160,1152]{1,0:T(8,128)(2,1)S(1)} collective-permute-done((bf16[160,1152]{1,0:T(8,128)(2,1)S(1)}, bf16[160,1152]{1,0:T(8,128)(2,1)S(1)}, u32[]{:S(2)}, u32[]{:S(2)}) %collective-permute-start.12) | collective-permute-done | bytes 368672 | tf_op jit(solution)/shard_map/ppermute | solution.py:578
  65.3 3.1 %collective-permute-start.19 = (bf16[160,1152]{1,0:T(8,128)(2,1)S(1)}, bf16[160,1152]{1,0:T(8,128)(2,1)S(1)}, u32[]{:S(2)}, u32[]{:S(2)}) collective-permute-start(bf16[160,1152]{1,0:T(8,128)(2,1)S(1)} %get-tuple-element.91), channel_id=1, source_target_pairs={{0,4},{1,5},{4,0},{5,1},{8,12},{9,13},{12,8},{13,9},{2,6},{3,7},{6... | collective-permute-start | bytes 1105928 | tf_op jit(solution)/shard_map/ppermute | solution.py:578
  68.4 4.6 %spread.2 = (bf16[16,320,1152]{2,1,0:T(8,128)(2,1)}, f32[8,128]{1,0:T(8,128)S(1)}) custom-call(bf16[512,256]{1,0:T(8,128)(2,1)S(1)} %mix.1.refs_2_.mix_ref, bf16[160,1152]{1,0:T(8,128)(2,1)S(1)} %get-tuple-element.85.refs_0_, bf16[160,1152]{1,0:T(8,128)(2,1)S(1)} %collective-permute-done.14.refs_1_, bf16[160,1152]{1,0:T(8,128)(2,1)S(1)} %collective-permute-done.15.refs_2_, ...), custom_call_target="tpu_custom_call" | custom-call | flops 1509949440 | bytes 5898240 | tf_op jit(solution)/shard_map/spread/pallas_call | solution.py:403
  73.5 5.1 %collective-permute-done.19.refs_1_ = bf16[160,1152]{1,0:T(8,128)(2,1)S(1)} collective-permute-done((bf16[160,1152]{1,0:T(8,128)(2,1)S(1)}, bf16[160,1152]{1,0:T(8,128)(2,1)S(1)}, u32[]{:S(2)}, u32[]{:S(2)}) %collective-permute-start.19) | collective-permute-done | bytes 368672 | tf_op jit(solution)/shard_map/ppermute | solution.py:578
  80.4 2.3 %collective-permute-start.21 = (bf16[160,1152]{1,0:T(8,128)(2,1)S(1)}, bf16[160,1152]{1,0:T(8,128)(2,1)S(1)}, u32[]{:S(2)}, u32[]{:S(2)}) collective-permute-start(bf16[160,1152]{1,0:T(8,128)(2,1)S(1)} %get-tuple-element.96), channel_id=1, source_target_pairs={{0,4},{1,5},{4,0},{5,1},{8,12},{9,13},{12,8},{13,9},{2,6},{3,7},{6... | collective-permute-start | bytes 1105928 | tf_op jit(solution)/shard_map/ppermute | solution.py:578
  82.8 4.9 %collective-permute-done.23.refs_1_ = bf16[160,1152]{1,0:T(8,128)(2,1)S(1)} collective-permute-done((bf16[160,1152]{1,0:T(8,128)(2,1)S(1)}, bf16[160,1152]{1,0:T(8,128)(2,1)S(1)}, u32[]{:S(2)}, u32[]{:S(2)}) %collective-permute-start.23) | collective-permute-done | bytes 368672 | tf_op jit(solution)/shard_map/ppermute | solution.py:519
  87.6 1.8 %columns.2 = (bf16[448,1280]{1,0:T(8,128)(2,1)}, f32[8,128]{1,0:T(8,128)S(1)}) custom-call(bf16[448,1152]{1,0:T(8,128)(2,1)S(1)} %get-tuple-element.53.live_ref, bf16[2720,1152]{1,0:T(8,128)(2,1)S(1)} %get-tuple-element.92.store_ref.refs_0_), custom_call_target="tpu_custom_call" | custom-call | flops 792723456 | bytes 688128 | tf_op jit(solution)/shard_map/columns/pallas_call | solution.py:271
  91.5 4.6 %spread.3 = (bf16[16,320,1152]{2,1,0:T(8,128)(2,1)}, f32[8,128]{1,0:T(8,128)S(1)}) custom-call(bf16[512,256]{1,0:T(8,128)(2,1)S(1)} %mix.1.refs_2_.mix_ref, bf16[160,1152]{1,0:T(8,128)(2,1)S(1)} %get-tuple-element.98.refs_0_, bf16[160,1152]{1,0:T(8,128)(2,1)S(1)} %collective-permute-done.23.refs_1_, ...), custom_call_target="tpu_custom_call", output_to_operand_aliasing={{0}: (5, {})} | custom-call | flops 1509949440 | bytes 5898240 | tf_op jit(solution)/shard_map/spread/pallas_call | solution.py:403
  96.1 4.6 %collective-permute-done.22.refs_1_ = bf16[160,1152]{1,0:T(8,128)(2,1)S(1)} collective-permute-done((bf16[160,1152]{1,0:T(8,128)(2,1)S(1)}, bf16[160,1152]{1,0:T(8,128)(2,1)S(1)}, u32[]{:S(2)}, u32[]{:S(2)}) %collective-permute-start.22) | collective-permute-done | bytes 368672 | tf_op jit(solution)/shard_map/ppermute | solution.py:578
  100.8 2.2 %columns.3 = (bf16[448,1280]{1,0:T(8,128)(2,1)}, f32[8,128]{1,0:T(8,128)}) custom-call(bf16[448,1152]{1,0:T(8,128)(2,1)S(1)} %get-tuple-element.53.live_ref, bf16[2720,1152]{1,0:T(8,128)(2,1)S(1)} %hop.55.store_ref, bf16[448,1280]{1,0:T(8,128)(2,1)} %get-tuple-element.101.refs_0_), custom_call_target="tpu_custom_call", output_to_operand_aliasing={{0}: (2, {})} | custom-call | flops 528482304 | bytes 458752 | tf_op jit(solution)/shard_map/columns/pallas_call | solution.py:271
  (77 shorter events, 18.8 us)
Async XLA Ops:
  3.9 12.1 %collective-permute-start = (bf16[160,1152]{1,0:T(8,128)(2,1)}, bf16[160,1152]{1,0:T(8,128)(2,1)S(1)}, u32[]{:S(2)}, u32[]{:S(2)}) collective-permute-start(bf16[160,1152]{1,0:T(8,128)(2,1)} %ends.1), channel_id=1, source_target_pairs={{0,4},{1,5},{4,0},{5,1},{8,12},{9,13},{12,8},{13,9},{2,6},{3,7},{6... | collective-permute-start | bytes 1105928 | tf_op jit(solution)/shard_map/ppermute | solution.py:578
  14.1 10.1 %collective-permute-start.1 = (bf16[160,1152]{1,0:T(8,128)(2,1)S(1)}, bf16[160,1152]{1,0:T(8,128)(2,1)S(1)}, u32[]{:S(2)}, u32[]{:S(2)}) collective-permute-start(bf16[160,1152]{1,0:T(8,128)(2,1)S(1)} %get-tuple-element.57), channel_id=1, source_target_pairs={{0,4},{1,5},{4,0},{5,1},{8,12},{9,13},{12,8},{13,9},{2,6},{3,7},{6... | collective-permute-start | bytes 1105928 | tf_op jit(solution)/shard_map/ppermute | solution.py:578
  16.3 8.3 %collective-permute-start.2 = (bf16[160,1152]{1,0:T(8,128)(2,1)S(1)}, bf16[160,1152]{1,0:T(8,128)(2,1)S(1)}, u32[]{:S(2)}, u32[]{:S(2)}) collective-permute-start(bf16[160,1152]{1,0:T(8,128)(2,1)S(1)} %get-tuple-element.59), channel_id=1, source_target_pairs={{0,1},{1,0},{4,8},{5,9},{8,4},{9,5},{12,13},{13,12},{2,3},{3,2},{6... | collective-permute-start | bytes 1105928 | tf_op jit(solution)/shard_map/ppermute | solution.py:578
  21.6 11.2 %collective-permute-start.3 = (bf16[160,1152]{1,0:T(8,128)(2,1)S(1)}, bf16[160,1152]{1,0:T(8,128)(2,1)S(1)}, u32[]{:S(2)}, u32[]{:S(2)}) collective-permute-start(bf16[160,1152]{1,0:T(8,128)(2,1)S(1)} %get-tuple-element.62), channel_id=1, source_target_pairs={{0,2},{2,0},{1,3},{3,1},{4,6},{6,4},{5,7},{7,5},{8,10},{10,8},{9,1... | collective-permute-start | bytes 1105928 | tf_op jit(solution)/shard_map/ppermute | solution.py:474
  24.5 10.8 %collective-permute-start.4 = (bf16[160,1152]{1,0:T(8,128)(2,1)S(1)}, bf16[160,1152]{1,0:T(8,128)(2,1)S(1)}, u32[]{:S(2)}, u32[]{:S(2)}) collective-permute-start(bf16[160,1152]{1,0:T(8,128)(2,1)S(1)} %get-tuple-element.66), channel_id=1, source_target_pairs={{0,1},{1,0},{4,8},{5,9},{8,4},{9,5},{12,13},{13,12},{2,3},{3,2},{6... | collective-permute-start | bytes 1105928 | tf_op jit(solution)/shard_map/ppermute | solution.py:578
  24.8 11.0 %collective-permute-start.5 = (bf16[160,1152]{1,0:T(8,128)(2,1)S(1)}, bf16[160,1152]{1,0:T(8,128)(2,1)S(1)}, u32[]{:S(2)}, u32[]{:S(2)}) collective-permute-start(bf16[160,1152]{1,0:T(8,128)(2,1)S(1)} %get-tuple-element.67), channel_id=1, source_target_pairs={{0,4},{1,5},{4,0},{5,1},{8,12},{9,13},{12,8},{13,9},{2,6},{3,7},{6... | collective-permute-start | bytes 1105928 | tf_op jit(solution)/shard_map/ppermute | solution.py:578
  31.3 8.7 %collective-permute-start.6 = (bf16[160,1152]{1,0:T(8,128)(2,1)S(1)}, bf16[160,1152]{1,0:T(8,128)(2,1)S(1)}, u32[]{:S(2)}, u32[]{:S(2)}) collective-permute-start(bf16[160,1152]{1,0:T(8,128)(2,1)S(1)} %get-tuple-element.69), channel_id=1, source_target_pairs={{0,2},{2,0},{1,3},{3,1},{4,6},{6,4},{5,7},{7,5},{8,10},{10,8},{9,1... | collective-permute-start | bytes 1105928 | tf_op jit(solution)/shard_map/ppermute | solution.py:474
  33.2 11.0 %collective-permute-start.8 = (bf16[160,1152]{1,0:T(8,128)(2,1)S(1)}, bf16[160,1152]{1,0:T(8,128)(2,1)S(1)}, u32[]{:S(2)}, u32[]{:S(2)}) collective-permute-start(bf16[160,1152]{1,0:T(8,128)(2,1)S(1)} %get-tuple-element.73), channel_id=1, source_target_pairs={{0,4},{1,5},{4,0},{5,1},{8,12},{9,13},{12,8},{13,9},{2,6},{3,7},{6... | collective-permute-start | bytes 1105928 | tf_op jit(solution)/shard_map/ppermute | solution.py:578
  36.1 10.6 %collective-permute-start.9 = (bf16[160,1152]{1,0:T(8,128)(2,1)S(1)}, bf16[160,1152]{1,0:T(8,128)(2,1)S(1)}, u32[]{:S(2)}, u32[]{:S(2)}) collective-permute-start(bf16[160,1152]{1,0:T(8,128)(2,1)S(1)} %get-tuple-element.75), channel_id=1, source_target_pairs={{0,1},{1,0},{4,8},{5,9},{8,4},{9,5},{12,13},{13,12},{2,3},{3,2},{6... | collective-permute-start | bytes 1105928 | tf_op jit(solution)/shard_map/ppermute | solution.py:578
  44.5 10.2 %collective-permute-start.14 = (bf16[160,1152]{1,0:T(8,128)(2,1)S(1)}, bf16[160,1152]{1,0:T(8,128)(2,1)S(1)}, u32[]{:S(2)}, u32[]{:S(2)}) collective-permute-start(bf16[160,1152]{1,0:T(8,128)(2,1)S(1)} %get-tuple-element.85.refs_0_), channel_id=1, source_target_pairs={{0,2},{2,0},{1,3},{3,1},{4,6},{6,4},{5,7},{7,5},{8,10},{10,8},{9,1... | collective-permute-start | bytes 1105928 | tf_op jit(solution)/shard_map/ppermute | solution.py:519
  45.6 11.5 %collective-permute-start.10 = (bf16[160,1152]{1,0:T(8,128)(2,1)S(1)}, bf16[160,1152]{1,0:T(8,128)(2,1)S(1)}, u32[]{:S(2)}, u32[]{:S(2)}) collective-permute-start(bf16[160,1152]{1,0:T(8,128)(2,1)S(1)} %get-tuple-element.77), channel_id=1, source_target_pairs={{0,4},{1,5},{4,0},{5,1},{8,12},{9,13},{12,8},{13,9},{2,6},{3,7},{6... | collective-permute-start | bytes 1105928 | tf_op jit(solution)/shard_map/ppermute | solution.py:578
  46.6 11.2 %collective-permute-start.11 = (bf16[160,1152]{1,0:T(8,128)(2,1)S(1)}, bf16[160,1152]{1,0:T(8,128)(2,1)S(1)}, u32[]{:S(2)}, u32[]{:S(2)}) collective-permute-start(bf16[160,1152]{1,0:T(8,128)(2,1)S(1)} %get-tuple-element.80), channel_id=1, source_target_pairs={{0,1},{1,0},{4,8},{5,9},{8,4},{9,5},{12,13},{13,12},{2,3},{3,2},{6... | collective-permute-start | bytes 1105928 | tf_op jit(solution)/shard_map/ppermute | solution.py:578
  46.9 18.0 %collective-permute-start.12 = (bf16[160,1152]{1,0:T(8,128)(2,1)S(1)}, bf16[160,1152]{1,0:T(8,128)(2,1)S(1)}, u32[]{:S(2)}, u32[]{:S(2)}) collective-permute-start(bf16[160,1152]{1,0:T(8,128)(2,1)S(1)} %get-tuple-element.81), channel_id=1, source_target_pairs={{0,4},{1,5},{4,0},{5,1},{8,12},{9,13},{12,8},{13,9},{2,6},{3,7},{6... | collective-permute-start | bytes 1105928 | tf_op jit(solution)/shard_map/ppermute | solution.py:578
  52.8 12.6 %collective-permute-start.15 = (bf16[160,1152]{1,0:T(8,128)(2,1)S(1)}, bf16[160,1152]{1,0:T(8,128)(2,1)S(1)}, u32[]{:S(2)}, u32[]{:S(2)}) collective-permute-start(bf16[160,1152]{1,0:T(8,128)(2,1)S(1)} %get-tuple-element.85.refs_0_), channel_id=1, source_target_pairs={{0,1},{1,0},{2,3},{3,2},{4,5},{5,4},{6,7},{7,6},{8,9},{9,8},{10,11... | collective-permute-start | bytes 1105928 | tf_op jit(solution)/shard_map/ppermute | solution.py:522
  54.7 13.8 %collective-permute-start.16 = (bf16[160,1152]{1,0:T(8,128)(2,1)S(1)}, bf16[160,1152]{1,0:T(8,128)(2,1)S(1)}, u32[]{:S(2)}, u32[]{:S(2)}) collective-permute-start(bf16[160,1152]{1,0:T(8,128)(2,1)S(1)} %collective-permute-done.14.refs_1_), channel_id=1, source_target_pairs={{0,1},{1,0},{2,3},{3,2},{4,5},{5,4},{6,7},{7,6},{8,9},{9,8},{10,11... | collective-permute-start | bytes 1105928 | tf_op jit(solution)/shard_map/ppermute | solution.py:522
  57.4 15.8 %collective-permute-start.17 = (bf16[160,1152]{1,0:T(8,128)(2,1)S(1)}, bf16[160,1152]{1,0:T(8,128)(2,1)S(1)}, u32[]{:S(2)}, u32[]{:S(2)}) collective-permute-start(bf16[160,1152]{1,0:T(8,128)(2,1)S(1)} %get-tuple-element.87), channel_id=1, source_target_pairs={{0,4},{1,5},{4,0},{5,1},{8,12},{9,13},{12,8},{13,9},{2,6},{3,7},{6... | collective-permute-start | bytes 1105928 | tf_op jit(solution)/shard_map/ppermute | solution.py:578
  57.8 15.2 %collective-permute-start.13 = (bf16[160,1152]{1,0:T(8,128)(2,1)S(1)}, bf16[160,1152]{1,0:T(8,128)(2,1)S(1)}, u32[]{:S(2)}, u32[]{:S(2)}) collective-permute-start(bf16[160,1152]{1,0:T(8,128)(2,1)S(1)} %get-tuple-element.84), channel_id=1, source_target_pairs={{0,1},{1,0},{4,8},{5,9},{8,4},{9,5},{12,13},{13,12},{2,3},{3,2},{6... | collective-permute-start | bytes 1105928 | tf_op jit(solution)/shard_map/ppermute | solution.py:578
  65.2 8.2 %collective-permute-start.18 = (bf16[160,1152]{1,0:T(8,128)(2,1)S(1)}, bf16[160,1152]{1,0:T(8,128)(2,1)S(1)}, u32[]{:S(2)}, u32[]{:S(2)}) collective-permute-start(bf16[160,1152]{1,0:T(8,128)(2,1)S(1)} %get-tuple-element.89), channel_id=1, source_target_pairs={{0,1},{1,0},{4,8},{5,9},{8,4},{9,5},{12,13},{13,12},{2,3},{3,2},{6... | collective-permute-start | bytes 1105928 | tf_op jit(solution)/shard_map/ppermute | solution.py:578
  65.3 13.3 %collective-permute-start.19 = (bf16[160,1152]{1,0:T(8,128)(2,1)S(1)}, bf16[160,1152]{1,0:T(8,128)(2,1)S(1)}, u32[]{:S(2)}, u32[]{:S(2)}) collective-permute-start(bf16[160,1152]{1,0:T(8,128)(2,1)S(1)} %get-tuple-element.91), channel_id=1, source_target_pairs={{0,4},{1,5},{4,0},{5,1},{8,12},{9,13},{12,8},{13,9},{2,6},{3,7},{6... | collective-permute-start | bytes 1105928 | tf_op jit(solution)/shard_map/ppermute | solution.py:578
  78.9 8.8 %collective-permute-start.23 = (bf16[160,1152]{1,0:T(8,128)(2,1)S(1)}, bf16[160,1152]{1,0:T(8,128)(2,1)S(1)}, u32[]{:S(2)}, u32[]{:S(2)}) collective-permute-start(bf16[160,1152]{1,0:T(8,128)(2,1)S(1)} %get-tuple-element.98.refs_0_), channel_id=1, source_target_pairs={{0,2},{2,0},{1,3},{3,1},{4,6},{6,4},{5,7},{7,5},{8,10},{10,8},{9,1... | collective-permute-start | bytes 1105928 | tf_op jit(solution)/shard_map/ppermute | solution.py:519
  80.4 9.1 %collective-permute-start.20 = (bf16[160,1152]{1,0:T(8,128)(2,1)S(1)}, bf16[160,1152]{1,0:T(8,128)(2,1)S(1)}, u32[]{:S(2)}, u32[]{:S(2)}) collective-permute-start(bf16[160,1152]{1,0:T(8,128)(2,1)S(1)} %get-tuple-element.93), channel_id=1, source_target_pairs={{0,1},{1,0},{4,8},{5,9},{8,4},{9,5},{12,13},{13,12},{2,3},{3,2},{6... | collective-permute-start | bytes 1105928 | tf_op jit(solution)/shard_map/ppermute | solution.py:578
  80.4 11.0 %collective-permute-start.21 = (bf16[160,1152]{1,0:T(8,128)(2,1)S(1)}, bf16[160,1152]{1,0:T(8,128)(2,1)S(1)}, u32[]{:S(2)}, u32[]{:S(2)}) collective-permute-start(bf16[160,1152]{1,0:T(8,128)(2,1)S(1)} %get-tuple-element.96), channel_id=1, source_target_pairs={{0,4},{1,5},{4,0},{5,1},{8,12},{9,13},{12,8},{13,9},{2,6},{3,7},{6... | collective-permute-start | bytes 1105928 | tf_op jit(solution)/shard_map/ppermute | solution.py:578
  82.8 8.7 %collective-permute-start.24 = (bf16[160,1152]{1,0:T(8,128)(2,1)S(1)}, bf16[160,1152]{1,0:T(8,128)(2,1)S(1)}, u32[]{:S(2)}, u32[]{:S(2)}) collective-permute-start(bf16[160,1152]{1,0:T(8,128)(2,1)S(1)} %get-tuple-element.98.refs_0_), channel_id=1, source_target_pairs={{0,1},{1,0},{2,3},{3,2},{4,5},{5,4},{6,7},{7,6},{8,9},{9,8},{10,11... | collective-permute-start | bytes 1105928 | tf_op jit(solution)/shard_map/ppermute | solution.py:522
  89.6 11.1 %collective-permute-start.22 = (bf16[160,1152]{1,0:T(8,128)(2,1)S(1)}, bf16[160,1152]{1,0:T(8,128)(2,1)S(1)}, u32[]{:S(2)}, u32[]{:S(2)}) collective-permute-start(bf16[160,1152]{1,0:T(8,128)(2,1)S(1)} %get-tuple-element.97), channel_id=1, source_target_pairs={{0,4},{1,5},{4,0},{5,1},{8,12},{9,13},{12,8},{13,9},{2,6},{3,7},{6... | collective-permute-start | bytes 1105928 | tf_op jit(solution)/shard_map/ppermute | solution.py:578
  (8 other events, 28.0 us)

commit v3 on v2

--- a/solution.py
+++ b/solution.py
@@ -14,7 +14,7 @@
 SKIPPED = (4,)
 SUMS_FIRST, SUMS_CHUNK, ROWS_CHUNK, OWN_WEIGHT = 3, 1, 0, -0.7
 MERGED_AT = (6, 8)
-SPREAD_BEFORE = (17, 99)
+SPREAD_BEFORE = (15, 99)
 MIX_BEFORE = 12
 ENDS_GRANT = 62 << 20
 MERGES_TOGETHER = True
@@ -246,9 +246,11 @@
     )(counts, features, grad)
 
 
-def columns_kernel(width_in, firsts, live_ref, store_ref, *refs):
-    out_ref, token_ref, part, done = refs[-4:]
-    token_ref[...] = jnp.zeros_like(token_ref)
+def columns_kernel(width_in, firsts, aliased, live_ref, store_ref, *refs):
+    *outs, part, done = refs[aliased:]
+    out_ref = outs[0]
+    for token_ref in outs[1:]:
+        token_ref[...] = jnp.zeros_like(token_ref)
     count, _, tile = part.shape
     first = at_device(firsts)
     writes = []
@@ -264,18 +266,18 @@
         write.wait()
 
 
-def columns(live, store, product, width_in, firsts, count, tile):
+def columns(live, store, product, width_in, firsts, count, tile, token=True):
     edges, width = live.shape
     vmem = pl.BlockSpec(memory_space=pltpu.VMEM)
     keep = pl.BlockSpec(memory_space=pl.ANY)
     return pl.pallas_call(
-        functools.partial(columns_kernel, width_in, firsts),
+        functools.partial(columns_kernel, width_in, firsts, int(product is not None)),
         in_specs=[vmem, vmem] + ([] if product is None else [keep]),
-        out_specs=[keep, vmem],
+        out_specs=[keep, vmem][: 1 + token],
         out_shape=[
             jax.ShapeDtypeStruct((edges, width_in), jnp.bfloat16),
             jax.ShapeDtypeStruct((8, 128), jnp.float32),
-        ],
+        ][: 1 + token],
         input_output_aliases={} if product is None else {2: 0},
         scratch_shapes=[pltpu.VMEM((count, edges, tile), jnp.bfloat16), pltpu.SemaphoreType.DMA((count,))],
         compiler_params=pltpu.CompilerParams(vmem_limit_bytes=8 << 20),
@@ -578,13 +580,24 @@
         got[move] = lax.ppermute(message, ("edge", "sys"), swaps(at, edge_size, sys_size))
         pending.append(move)
         store, result = finish(store, result)
-    while pending:
-        (store,) = settle(store, pending[0], None, rows, list(tokens.values()) if len(pending) == 1 else ())
+    while len(pending) > 1:
+        (store,) = settle(store, pending[0], None, rows)
         store, result = finish(store, result)
-    rest = width_in // wide - tiles
+    rest, behind = width_in // wide - tiles, []
     if rest:
-        firsts_late = [0 if first else tiles * wide for first in firsts_early]
-        product, _ = columns(live, store, product, width_in, firsts_late, rest, wide)
+        firsts_rest = [0 if first else tiles * wide for first in firsts_early]
+        product, token = columns(live, store, product, width_in, firsts_rest, rest, wide)
+        behind.append(token)
+    last = [0] * edge_size
+    at, part = pending[0]
+    for _, target, kind, b, h, _ in steps[at]:
+        if kind == "M":
+            last[target] = b * row_count + extent(h, part)[0]
+    span = min(width_in, max(-(-(first % 128 + extent(0, part)[1]) // 128) * 128 for first in last))
+    firsts_last = [min(first // 128 * 128, width_in - span) for first in last]
+    (store,) = settle(store, pending[0], None, rows, behind + list(tokens.values()))
+    store, result = finish(store, result)
+    (product,) = columns(live, store, product, width_in, firsts_last, 1, span, token=False)
     return (product[None], result)
 
 

time: 103 us -> 108 us (1.049)
  waiting for transfers between devices: 37.7 us -> 42.2 us
    ppermute x2, waiting for transfers between devices: 6.74 us -> 11.2 us  [finish(): column.append(lax.ppermute(rows_h, 'expert', shift(expert_size, k)))]
    ppermute x18, waiting for transfers between devices: 27.1 us -> 28.6 us  [body(): lax.ppermute(message, ('edge', 'sys'), swaps(at, edge_size, sys_size))]
    ppermute x2, waiting for transfers between devices: 3.8 us -> 2.35 us  [body(): lax.ppermute(parts[k], 'expert', shift(expert_size, k))]
    pallas_call x2 -> x3, Pallas kernels: 4 us -> 4.62 us  [columns(): pl.pallas_call(functools.partial(columns_kernel, width_in, firsts, int(pr...]
  transfers between devices with their start and end apart: 26 -> 26, of which waited for: 12 -> 11; matrix products, arithmetic and copies ran while one was open for 0% -> 0% of each run, Pallas kernels for 25% -> 25%
where the time goes in v3:
time: 108 us
  waiting for transfers between devices  42.2 us (39%)
  Pallas kernels  32.2 us (30%)
  starting transfers between devices  27.1 us (25%)
  local copies, waits for them, and re-layouts  5.15 us (5%)
    ppermute x18, waiting for transfers between devices, body(): lax.ppermute(message, ('edge', 'sys'), swaps(at, edge_size, sys_size))  28.6 us
    ppermute x18, starting transfers between devices, body(): lax.ppermute(message, ('edge', 'sys'), swaps(at, edge_size, sys_size))  21.8 us
    ppermute x2, waiting for transfers between devices, finish(): column.append(lax.ppermute(rows_h, 'expert', shift(expert_size, k)))  11.2 us
    pallas_call x2, Pallas kernels, spread(): pl.pallas_call(functools.partial(spread_kernel, count, groups), grid=(row...  9.24 us
    pallas_call x2, Pallas kernels, merge_part(): pl.pallas_call(functools.partial(merge_kernel, expert_size, sys_size, fir...  6.5 us
    unnamed x12, local copies, waits for them, and re-layouts  5.15 us
    pallas_call x3, Pallas kernels, columns(): pl.pallas_call(functools.partial(columns_kernel, width_in, firsts, int(pr...  4.62 us
    pallas_call x28, Pallas kernels, hop(): pl.pallas_call(functools.partial(hop_kernel, len(arrays), len(behind), ta...  3.9 us
  transfers between devices with their start and end apart: 26, of which 11 were waited for; matrix products, arithmetic and copies ran while one was open for 0% of the time, Pallas kernels for 25%

profile of v3, /device:TPU:0, one launch (start us, length us, event | category | flops | bytes accessed | tf_op | source)
XLA Modules:
  0.0 107.7 jit_solution(3805811654790293379)
XLA Ops:
  0.6 3.3 %ends.1 = bf16[160,1152]{1,0:T(8,128)(2,1)} custom-call(s32[4]{0:T(128)} %counts_ref.3, bf16[448,1280]{1,0:T(8,128)(2,1)} %bitcast.3, bf16[448,1152]{1,0:T(8,128)(2,1)} %bitcast.5), custom_call_target="tpu_custom_call" | custom-call | flops 264241152 | bytes 1261568 | tf_op jit(solution)/shard_map/ends/pallas_call | solution.py:186
  3.9 3.1 %collective-permute-start = (bf16[160,1152]{1,0:T(8,128)(2,1)}, bf16[160,1152]{1,0:T(8,128)(2,1)S(1)}, u32[]{:S(2)}, u32[]{:S(2)}) collective-permute-start(bf16[160,1152]{1,0:T(8,128)(2,1)} %ends.1), channel_id=1, source_target_pairs={{0,4},{1,5},{4,0},{5,1},{8,12},{9,13},{12,8},{13,9},{2,6},{3,7},{6... | collective-permute-start | bytes 1105928 | tf_op jit(solution)/shard_map/ppermute | solution.py:580
  10.1 3.9 %outer.1 = (bf16[2720,1152]{1,0:T(8,128)(2,1)S(1)}, bf16[448,1152]{1,0:T(8,128)(2,1)S(1)}) custom-call(s32[4]{0:T(128)S(1)} %copy-done.5, bf16[448,1280]{1,0:T(8,128)(2,1)S(1)} %bitcast.4, bf16[448,1152]{1,0:T(8,128)(2,1)S(1)} %bitcast.6), custom_call_target="tpu_custom_call" | custom-call | flops 1321205760 | bytes 5128192 | tf_op jit(solution)/shard_map/outer/pallas_call | solution.py:223
  14.2 1.8 %collective-permute-done.refs_1_ = bf16[160,1152]{1,0:T(8,128)(2,1)S(1)} collective-permute-done((bf16[160,1152]{1,0:T(8,128)(2,1)}, bf16[160,1152]{1,0:T(8,128)(2,1)S(1)}, u32[]{:S(2)}, u32[]{:S(2)}) %collective-permute-start) | collective-permute-done | bytes 368672 | tf_op jit(solution)/shard_map/ppermute | solution.py:580
  16.4 2.0 %copy-done = bf16[16,320,1152]{2,1,0:T(8,128)(2,1)S(1)} copy-done((bf16[16,320,1152]{2,1,0:T(8,128)(2,1)S(1)}, bf16[16,320,1152]{2,1,0:T(8,128)(2,1)}, u32[]{:S(2)}) %copy-start) | copy-done | bytes 11796504
  18.4 3.3 %merge.2 = (bf16[160,1152]{1,0:T(8,128)(2,1)S(1)}, bf16[160,1152]{1,0:T(8,128)(2,1)S(1)}) custom-call(f32[16,32]{1,0:T(8,128)S(1)} %copy-done.3, s32[4]{0:T(128)S(1)} %copy-done.4, bf16[16,320,1152]{2,1,0:T(8,128)(2,1)S(1)} %copy-done), custom_call_target="tpu_custom_call" | custom-call | flops 11796480 | bytes 5898240 | tf_op jit(solution)/shard_map/merge/pallas_call | solution.py:129
  23.2 3.2 %merge.3 = (bf16[160,1152]{1,0:T(8,128)(2,1)S(1)}, bf16[160,1152]{1,0:T(8,128)(2,1)S(1)}) custom-call(f32[16,32]{1,0:T(8,128)S(1)} %copy-done.3, s32[4]{0:T(128)S(1)} %copy-done.4, bf16[16,320,1152]{2,1,0:T(8,128)(2,1)S(1)} %copy-done), custom_call_target="tpu_custom_call" | custom-call | flops 11796480 | bytes 5898240 | tf_op jit(solution)/shard_map/merge/pallas_call | solution.py:129
  27.6 3.2 %collective-permute-start.5 = (bf16[160,1152]{1,0:T(8,128)(2,1)S(1)}, bf16[160,1152]{1,0:T(8,128)(2,1)S(1)}, u32[]{:S(2)}, u32[]{:S(2)}) collective-permute-start(bf16[160,1152]{1,0:T(8,128)(2,1)S(1)} %get-tuple-element.68), channel_id=1, source_target_pairs={{0,4},{1,5},{4,0},{5,1},{8,12},{9,13},{12,8},{13,9},{2,6},{3,7},{6... | collective-permute-start | bytes 1105928 | tf_op jit(solution)/shard_map/ppermute | solution.py:580
  30.8 2.4 %collective-permute-done.3.refs_2_ = bf16[160,1152]{1,0:T(8,128)(2,1)S(1)} collective-permute-done((bf16[160,1152]{1,0:T(8,128)(2,1)S(1)}, bf16[160,1152]{1,0:T(8,128)(2,1)S(1)}, u32[]{:S(2)}, u32[]{:S(2)}) %collective-permute-start.3) | collective-permute-done | bytes 368672 | tf_op jit(solution)/shard_map/ppermute | solution.py:476
  33.5 3.2 %collective-permute-start.8 = (bf16[160,1152]{1,0:T(8,128)(2,1)S(1)}, bf16[160,1152]{1,0:T(8,128)(2,1)S(1)}, u32[]{:S(2)}, u32[]{:S(2)}) collective-permute-start(bf16[160,1152]{1,0:T(8,128)(2,1)S(1)} %get-tuple-element.74), channel_id=1, source_target_pairs={{0,4},{1,5},{4,0},{5,1},{8,12},{9,13},{12,8},{13,9},{2,6},{3,7},{6... | collective-permute-start | bytes 1105928 | tf_op jit(solution)/shard_map/ppermute | solution.py:580
  36.9 3.3 %collective-permute-done.5.refs_1_ = bf16[160,1152]{1,0:T(8,128)(2,1)S(1)} collective-permute-done((bf16[160,1152]{1,0:T(8,128)(2,1)S(1)}, bf16[160,1152]{1,0:T(8,128)(2,1)S(1)}, u32[]{:S(2)}, u32[]{:S(2)}) %collective-permute-start.5) | collective-permute-done | bytes 368672 | tf_op jit(solution)/shard_map/ppermute | solution.py:580
  41.7 4.9 %collective-permute-done.8.refs_1_ = bf16[160,1152]{1,0:T(8,128)(2,1)S(1)} collective-permute-done((bf16[160,1152]{1,0:T(8,128)(2,1)S(1)}, bf16[160,1152]{1,0:T(8,128)(2,1)S(1)}, u32[]{:S(2)}, u32[]{:S(2)}) %collective-permute-start.8) | collective-permute-done | bytes 368672 | tf_op jit(solution)/shard_map/ppermute | solution.py:580
  48.4 1.9 %collective-permute-start.10 = (bf16[160,1152]{1,0:T(8,128)(2,1)S(1)}, bf16[160,1152]{1,0:T(8,128)(2,1)S(1)}, u32[]{:S(2)}, u32[]{:S(2)}) collective-permute-start(bf16[160,1152]{1,0:T(8,128)(2,1)S(1)} %get-tuple-element.78), channel_id=1, source_target_pairs={{0,4},{1,5},{4,0},{5,1},{8,12},{9,13},{12,8},{13,9},{2,6},{3,7},{6... | collective-permute-start | bytes 1105928 | tf_op jit(solution)/shard_map/ppermute | solution.py:580
  50.2 5.7 %collective-permute-done.12.refs_1_ = bf16[160,1152]{1,0:T(8,128)(2,1)S(1)} collective-permute-done((bf16[160,1152]{1,0:T(8,128)(2,1)S(1)}, bf16[160,1152]{1,0:T(8,128)(2,1)S(1)}, u32[]{:S(2)}, u32[]{:S(2)}) %collective-permute-start.12) | collective-permute-done | bytes 368672 | tf_op jit(solution)/shard_map/ppermute | solution.py:521
  60.1 4.6 %spread.2 = (bf16[16,320,1152]{2,1,0:T(8,128)(2,1)}, f32[8,128]{1,0:T(8,128)S(1)}) custom-call(bf16[512,256]{1,0:T(8,128)(2,1)S(1)} %mix.1.refs_2_.mix_ref, bf16[160,1152]{1,0:T(8,128)(2,1)S(1)} %get-tuple-element.82.refs_0_, bf16[160,1152]{1,0:T(8,128)(2,1)S(1)} %collective-permute-done.12.refs_1_, bf16[160,1152]{1,0:T(8,128)(2,1)S(1)} %collective-permute-done.13.refs_2_, ...), custom_call_target="tpu_custom_call" | custom-call | flops 1509949440 | bytes 5898240 | tf_op jit(solution)/shard_map/spread/pallas_call | solution.py:405
  64.7 3.4 %collective-permute-done.15.refs_1_ = bf16[160,1152]{1,0:T(8,128)(2,1)S(1)} collective-permute-done((bf16[160,1152]{1,0:T(8,128)(2,1)S(1)}, bf16[160,1152]{1,0:T(8,128)(2,1)S(1)}, u32[]{:S(2)}, u32[]{:S(2)}) %collective-permute-start.15) | collective-permute-done | bytes 368672 | tf_op jit(solution)/shard_map/ppermute | solution.py:580
  68.6 2.9 %collective-permute-start.19 = (bf16[160,1152]{1,0:T(8,128)(2,1)S(1)}, bf16[160,1152]{1,0:T(8,128)(2,1)S(1)}, u32[]{:S(2)}, u32[]{:S(2)}) collective-permute-start(bf16[160,1152]{1,0:T(8,128)(2,1)S(1)} %get-tuple-element.92), channel_id=1, source_target_pairs={{0,4},{1,5},{4,0},{5,1},{8,12},{9,13},{12,8},{13,9},{2,6},{3,7},{6... | collective-permute-start | bytes 1105928 | tf_op jit(solution)/shard_map/ppermute | solution.py:580
  71.7 4.4 %collective-permute-done.17.refs_1_ = bf16[160,1152]{1,0:T(8,128)(2,1)S(1)} collective-permute-done((bf16[160,1152]{1,0:T(8,128)(2,1)S(1)}, bf16[160,1152]{1,0:T(8,128)(2,1)S(1)}, u32[]{:S(2)}, u32[]{:S(2)}) %collective-permute-start.17) | collective-permute-done | bytes 368672 | tf_op jit(solution)/shard_map/ppermute | solution.py:580
  76.4 6.8 %collective-permute-done.19.refs_1_ = bf16[160,1152]{1,0:T(8,128)(2,1)S(1)} collective-permute-done((bf16[160,1152]{1,0:T(8,128)(2,1)S(1)}, bf16[160,1152]{1,0:T(8,128)(2,1)S(1)}, u32[]{:S(2)}, u32[]{:S(2)}) %collective-permute-start.19) | collective-permute-done | bytes 368672 | tf_op jit(solution)/shard_map/ppermute | solution.py:580
  85.0 2.8 %collective-permute-start.21 = (bf16[160,1152]{1,0:T(8,128)(2,1)S(1)}, bf16[160,1152]{1,0:T(8,128)(2,1)S(1)}, u32[]{:S(2)}, u32[]{:S(2)}) collective-permute-start(bf16[160,1152]{1,0:T(8,128)(2,1)S(1)} %get-tuple-element.97), channel_id=1, source_target_pairs={{0,4},{1,5},{4,0},{5,1},{8,12},{9,13},{12,8},{13,9},{2,6},{3,7},{6... | collective-permute-start | bytes 1105928 | tf_op jit(solution)/shard_map/ppermute | solution.py:580
  87.8 5.6 %collective-permute-done.23.refs_1_ = bf16[160,1152]{1,0:T(8,128)(2,1)S(1)} collective-permute-done((bf16[160,1152]{1,0:T(8,128)(2,1)S(1)}, bf16[160,1152]{1,0:T(8,128)(2,1)S(1)}, u32[]{:S(2)}, u32[]{:S(2)}) %collective-permute-start.23) | collective-permute-done | bytes 368672 | tf_op jit(solution)/shard_map/ppermute | solution.py:521
  95.3 1.8 %collective-permute-start.22 = (bf16[160,1152]{1,0:T(8,128)(2,1)S(1)}, bf16[160,1152]{1,0:T(8,128)(2,1)S(1)}, u32[]{:S(2)}, u32[]{:S(2)}) collective-permute-start(bf16[160,1152]{1,0:T(8,128)(2,1)S(1)} %get-tuple-element.98), channel_id=1, source_target_pairs={{0,4},{1,5},{4,0},{5,1},{8,12},{9,13},{12,8},{13,9},{2,6},{3,7},{6... | collective-permute-start | bytes 1105928 | tf_op jit(solution)/shard_map/ppermute | solution.py:580
  98.9 4.6 %spread.3 = (bf16[16,320,1152]{2,1,0:T(8,128)(2,1)}, f32[8,128]{1,0:T(8,128)S(1)}) custom-call(bf16[512,256]{1,0:T(8,128)(2,1)S(1)} %mix.1.refs_2_.mix_ref, bf16[160,1152]{1,0:T(8,128)(2,1)S(1)} %get-tuple-element.101.refs_0_, bf16[160,1152]{1,0:T(8,128)(2,1)S(1)} %collective-permute-done.23.refs_1_, ...), custom_call_target="tpu_custom_call", output_to_operand_aliasing={{0}: (5, {})} | custom-call | flops 1509949440 | bytes 5898240 | tf_op jit(solution)/shard_map/spread/pallas_call | solution.py:405
  103.5 3.0 %collective-permute-done.22.refs_1_ = bf16[160,1152]{1,0:T(8,128)(2,1)S(1)} collective-permute-done((bf16[160,1152]{1,0:T(8,128)(2,1)S(1)}, bf16[160,1152]{1,0:T(8,128)(2,1)S(1)}, u32[]{:S(2)}, u32[]{:S(2)}) %collective-permute-start.22) | collective-permute-done | bytes 368672 | tf_op jit(solution)/shard_map/ppermute | solution.py:580
  (78 shorter events, 21.8 us)
Async XLA Ops:
  3.9 12.1 %collective-permute-start = (bf16[160,1152]{1,0:T(8,128)(2,1)}, bf16[160,1152]{1,0:T(8,128)(2,1)S(1)}, u32[]{:S(2)}, u32[]{:S(2)}) collective-permute-start(bf16[160,1152]{1,0:T(8,128)(2,1)} %ends.1), channel_id=1, source_target_pairs={{0,4},{1,5},{4,0},{5,1},{8,12},{9,13},{12,8},{13,9},{2,6},{3,7},{6... | collective-permute-start | bytes 1105928 | tf_op jit(solution)/shard_map/ppermute | solution.py:580
  14.1 12.9 %collective-permute-start.1 = (bf16[160,1152]{1,0:T(8,128)(2,1)S(1)}, bf16[160,1152]{1,0:T(8,128)(2,1)S(1)}, u32[]{:S(2)}, u32[]{:S(2)}) collective-permute-start(bf16[160,1152]{1,0:T(8,128)(2,1)S(1)} %get-tuple-element.58), channel_id=1, source_target_pairs={{0,4},{1,5},{4,0},{5,1},{8,12},{9,13},{12,8},{13,9},{2,6},{3,7},{6... | collective-permute-start | bytes 1105928 | tf_op jit(solution)/shard_map/ppermute | solution.py:580
  16.3 11.1 %collective-permute-start.2 = (bf16[160,1152]{1,0:T(8,128)(2,1)S(1)}, bf16[160,1152]{1,0:T(8,128)(2,1)S(1)}, u32[]{:S(2)}, u32[]{:S(2)}) collective-permute-start(bf16[160,1152]{1,0:T(8,128)(2,1)S(1)} %get-tuple-element.60), channel_id=1, source_target_pairs={{0,1},{1,0},{4,8},{5,9},{8,4},{9,5},{12,13},{13,12},{2,3},{3,2},{6... | collective-permute-start | bytes 1105928 | tf_op jit(solution)/shard_map/ppermute | solution.py:580
  21.6 11.5 %collective-permute-start.3 = (bf16[160,1152]{1,0:T(8,128)(2,1)S(1)}, bf16[160,1152]{1,0:T(8,128)(2,1)S(1)}, u32[]{:S(2)}, u32[]{:S(2)}) collective-permute-start(bf16[160,1152]{1,0:T(8,128)(2,1)S(1)} %get-tuple-element.63), channel_id=1, source_target_pairs={{0,2},{2,0},{1,3},{3,1},{4,6},{6,4},{5,7},{7,5},{8,10},{10,8},{9,1... | collective-permute-start | bytes 1105928 | tf_op jit(solution)/shard_map/ppermute | solution.py:476
  26.4 14.0 %collective-permute-start.6 = (bf16[160,1152]{1,0:T(8,128)(2,1)S(1)}, bf16[160,1152]{1,0:T(8,128)(2,1)S(1)}, u32[]{:S(2)}, u32[]{:S(2)}) collective-permute-start(bf16[160,1152]{1,0:T(8,128)(2,1)S(1)} %get-tuple-element.70), channel_id=1, source_target_pairs={{0,2},{2,0},{1,3},{3,1},{4,6},{6,4},{5,7},{7,5},{8,10},{10,8},{9,1... | collective-permute-start | bytes 1105928 | tf_op jit(solution)/shard_map/ppermute | solution.py:476
  27.3 9.5 %collective-permute-start.4 = (bf16[160,1152]{1,0:T(8,128)(2,1)S(1)}, bf16[160,1152]{1,0:T(8,128)(2,1)S(1)}, u32[]{:S(2)}, u32[]{:S(2)}) collective-permute-start(bf16[160,1152]{1,0:T(8,128)(2,1)S(1)} %get-tuple-element.67), channel_id=1, source_target_pairs={{0,1},{1,0},{4,8},{5,9},{8,4},{9,5},{12,13},{13,12},{2,3},{3,2},{6... | collective-permute-start | bytes 1105928 | tf_op jit(solution)/shard_map/ppermute | solution.py:580
  27.6 12.6 %collective-permute-start.5 = (bf16[160,1152]{1,0:T(8,128)(2,1)S(1)}, bf16[160,1152]{1,0:T(8,128)(2,1)S(1)}, u32[]{:S(2)}, u32[]{:S(2)}) collective-permute-start(bf16[160,1152]{1,0:T(8,128)(2,1)S(1)} %get-tuple-element.68), channel_id=1, source_target_pairs={{0,4},{1,5},{4,0},{5,1},{8,12},{9,13},{12,8},{13,9},{2,6},{3,7},{6... | collective-permute-start | bytes 1105928 | tf_op jit(solution)/shard_map/ppermute | solution.py:580
  33.4 8.2 %collective-permute-start.7 = (bf16[160,1152]{1,0:T(8,128)(2,1)S(1)}, bf16[160,1152]{1,0:T(8,128)(2,1)S(1)}, u32[]{:S(2)}, u32[]{:S(2)}) collective-permute-start(bf16[160,1152]{1,0:T(8,128)(2,1)S(1)} %get-tuple-element.72), channel_id=1, source_target_pairs={{0,1},{1,0},{4,8},{5,9},{8,4},{9,5},{12,13},{13,12},{2,3},{3,2},{6... | collective-permute-start | bytes 1105928 | tf_op jit(solution)/shard_map/ppermute | solution.py:580
  33.5 13.0 %collective-permute-start.8 = (bf16[160,1152]{1,0:T(8,128)(2,1)S(1)}, bf16[160,1152]{1,0:T(8,128)(2,1)S(1)}, u32[]{:S(2)}, u32[]{:S(2)}) collective-permute-start(bf16[160,1152]{1,0:T(8,128)(2,1)S(1)} %get-tuple-element.74), channel_id=1, source_target_pairs={{0,4},{1,5},{4,0},{5,1},{8,12},{9,13},{12,8},{13,9},{2,6},{3,7},{6... | collective-permute-start | bytes 1105928 | tf_op jit(solution)/shard_map/ppermute | solution.py:580
  46.8 9.1 %collective-permute-start.12 = (bf16[160,1152]{1,0:T(8,128)(2,1)S(1)}, bf16[160,1152]{1,0:T(8,128)(2,1)S(1)}, u32[]{:S(2)}, u32[]{:S(2)}) collective-permute-start(bf16[160,1152]{1,0:T(8,128)(2,1)S(1)} %get-tuple-element.82.refs_0_), channel_id=1, source_target_pairs={{0,2},{2,0},{1,3},{3,1},{4,6},{6,4},{5,7},{7,5},{8,10},{10,8},{9,1... | collective-permute-start | bytes 1105928 | tf_op jit(solution)/shard_map/ppermute | solution.py:521
  48.4 8.0 %collective-permute-start.9 = (bf16[160,1152]{1,0:T(8,128)(2,1)S(1)}, bf16[160,1152]{1,0:T(8,128)(2,1)S(1)}, u32[]{:S(2)}, u32[]{:S(2)}) collective-permute-start(bf16[160,1152]{1,0:T(8,128)(2,1)S(1)} %get-tuple-element.76), channel_id=1, source_target_pairs={{0,1},{1,0},{4,8},{5,9},{8,4},{9,5},{12,13},{13,12},{2,3},{3,2},{6... | collective-permute-start | bytes 1105928 | tf_op jit(solution)/shard_map/ppermute | solution.py:580
  48.4 11.0 %collective-permute-start.10 = (bf16[160,1152]{1,0:T(8,128)(2,1)S(1)}, bf16[160,1152]{1,0:T(8,128)(2,1)S(1)}, u32[]{:S(2)}, u32[]{:S(2)}) collective-permute-start(bf16[160,1152]{1,0:T(8,128)(2,1)S(1)} %get-tuple-element.78), channel_id=1, source_target_pairs={{0,4},{1,5},{4,0},{5,1},{8,12},{9,13},{12,8},{13,9},{2,6},{3,7},{6... | collective-permute-start | bytes 1105928 | tf_op jit(solution)/shard_map/ppermute | solution.py:580
  50.2 9.8 %collective-permute-start.13 = (bf16[160,1152]{1,0:T(8,128)(2,1)S(1)}, bf16[160,1152]{1,0:T(8,128)(2,1)S(1)}, u32[]{:S(2)}, u32[]{:S(2)}) collective-permute-start(bf16[160,1152]{1,0:T(8,128)(2,1)S(1)} %get-tuple-element.82.refs_0_), channel_id=1, source_target_pairs={{0,1},{1,0},{2,3},{3,2},{4,5},{5,4},{6,7},{7,6},{8,9},{9,8},{10,11... | collective-permute-start | bytes 1105928 | tf_op jit(solution)/shard_map/ppermute | solution.py:524
  55.9 8.8 %collective-permute-start.11 = (bf16[160,1152]{1,0:T(8,128)(2,1)S(1)}, bf16[160,1152]{1,0:T(8,128)(2,1)S(1)}, u32[]{:S(2)}, u32[]{:S(2)}) collective-permute-start(bf16[160,1152]{1,0:T(8,128)(2,1)S(1)} %get-tuple-element.81), channel_id=1, source_target_pairs={{0,1},{1,0},{4,8},{5,9},{8,4},{9,5},{12,13},{13,12},{2,3},{3,2},{6... | collective-permute-start | bytes 1105928 | tf_op jit(solution)/shard_map/ppermute | solution.py:580
  56.6 11.5 %collective-permute-start.15 = (bf16[160,1152]{1,0:T(8,128)(2,1)S(1)}, bf16[160,1152]{1,0:T(8,128)(2,1)S(1)}, u32[]{:S(2)}, u32[]{:S(2)}) collective-permute-start(bf16[160,1152]{1,0:T(8,128)(2,1)S(1)} %get-tuple-element.84), channel_id=1, source_target_pairs={{0,4},{1,5},{4,0},{5,1},{8,12},{9,13},{12,8},{13,9},{2,6},{3,7},{6... | collective-permute-start | bytes 1105928 | tf_op jit(solution)/shard_map/ppermute | solution.py:580
  59.7 16.4 %collective-permute-start.17 = (bf16[160,1152]{1,0:T(8,128)(2,1)S(1)}, bf16[160,1152]{1,0:T(8,128)(2,1)S(1)}, u32[]{:S(2)}, u32[]{:S(2)}) collective-permute-start(bf16[160,1152]{1,0:T(8,128)(2,1)S(1)} %get-tuple-element.88), channel_id=1, source_target_pairs={{0,4},{1,5},{4,0},{5,1},{8,12},{9,13},{12,8},{13,9},{2,6},{3,7},{6... | collective-permute-start | bytes 1105928 | tf_op jit(solution)/shard_map/ppermute | solution.py:580
  60.0 11.5 %collective-permute-start.16 = (bf16[160,1152]{1,0:T(8,128)(2,1)S(1)}, bf16[160,1152]{1,0:T(8,128)(2,1)S(1)}, u32[]{:S(2)}, u32[]{:S(2)}) collective-permute-start(bf16[160,1152]{1,0:T(8,128)(2,1)S(1)} %get-tuple-element.87), channel_id=1, source_target_pairs={{0,1},{1,0},{4,8},{5,9},{8,4},{9,5},{12,13},{13,12},{2,3},{3,2},{6... | collective-permute-start | bytes 1105928 | tf_op jit(solution)/shard_map/ppermute | solution.py:580
  68.4 7.8 %collective-permute-start.18 = (bf16[160,1152]{1,0:T(8,128)(2,1)S(1)}, bf16[160,1152]{1,0:T(8,128)(2,1)S(1)}, u32[]{:S(2)}, u32[]{:S(2)}) collective-permute-start(bf16[160,1152]{1,0:T(8,128)(2,1)S(1)} %get-tuple-element.90), channel_id=1, source_target_pairs={{0,1},{1,0},{4,8},{5,9},{8,4},{9,5},{12,13},{13,12},{2,3},{3,2},{6... | collective-permute-start | bytes 1105928 | tf_op jit(solution)/shard_map/ppermute | solution.py:580
  68.6 14.6 %collective-permute-start.19 = (bf16[160,1152]{1,0:T(8,128)(2,1)S(1)}, bf16[160,1152]{1,0:T(8,128)(2,1)S(1)}, u32[]{:S(2)}, u32[]{:S(2)}) collective-permute-start(bf16[160,1152]{1,0:T(8,128)(2,1)S(1)} %get-tuple-element.92), channel_id=1, source_target_pairs={{0,4},{1,5},{4,0},{5,1},{8,12},{9,13},{12,8},{13,9},{2,6},{3,7},{6... | collective-permute-start | bytes 1105928 | tf_op jit(solution)/shard_map/ppermute | solution.py:580
  83.4 9.9 %collective-permute-start.23 = (bf16[160,1152]{1,0:T(8,128)(2,1)S(1)}, bf16[160,1152]{1,0:T(8,128)(2,1)S(1)}, u32[]{:S(2)}, u32[]{:S(2)}) collective-permute-start(bf16[160,1152]{1,0:T(8,128)(2,1)S(1)} %get-tuple-element.101.refs_0_), channel_id=1, source_target_pairs={{0,2},{2,0},{1,3},{3,1},{4,6},{6,4},{5,7},{7,5},{8,10},{10,8},{9,1... | collective-permute-start | bytes 1105928 | tf_op jit(solution)/shard_map/ppermute | solution.py:521
  85.0 10.2 %collective-permute-start.20 = (bf16[160,1152]{1,0:T(8,128)(2,1)S(1)}, bf16[160,1152]{1,0:T(8,128)(2,1)S(1)}, u32[]{:S(2)}, u32[]{:S(2)}) collective-permute-start(bf16[160,1152]{1,0:T(8,128)(2,1)S(1)} %get-tuple-element.94), channel_id=1, source_target_pairs={{0,1},{1,0},{4,8},{5,9},{8,4},{9,5},{12,13},{13,12},{2,3},{3,2},{6... | collective-permute-start | bytes 1105928 | tf_op jit(solution)/shard_map/ppermute | solution.py:580
  85.0 12.2 %collective-permute-start.21 = (bf16[160,1152]{1,0:T(8,128)(2,1)S(1)}, bf16[160,1152]{1,0:T(8,128)(2,1)S(1)}, u32[]{:S(2)}, u32[]{:S(2)}) collective-permute-start(bf16[160,1152]{1,0:T(8,128)(2,1)S(1)} %get-tuple-element.97), channel_id=1, source_target_pairs={{0,4},{1,5},{4,0},{5,1},{8,12},{9,13},{12,8},{13,9},{2,6},{3,7},{6... | collective-permute-start | bytes 1105928 | tf_op jit(solution)/shard_map/ppermute | solution.py:580
  87.8 11.1 %collective-permute-start.24 = (bf16[160,1152]{1,0:T(8,128)(2,1)S(1)}, bf16[160,1152]{1,0:T(8,128)(2,1)S(1)}, u32[]{:S(2)}, u32[]{:S(2)}) collective-permute-start(bf16[160,1152]{1,0:T(8,128)(2,1)S(1)} %get-tuple-element.101.refs_0_), channel_id=1, source_target_pairs={{0,1},{1,0},{2,3},{3,2},{4,5},{5,4},{6,7},{7,6},{8,9},{9,8},{10,11... | collective-permute-start | bytes 1105928 | tf_op jit(solution)/shard_map/ppermute | solution.py:524
  95.3 11.1 %collective-permute-start.22 = (bf16[160,1152]{1,0:T(8,128)(2,1)S(1)}, bf16[160,1152]{1,0:T(8,128)(2,1)S(1)}, u32[]{:S(2)}, u32[]{:S(2)}) collective-permute-start(bf16[160,1152]{1,0:T(8,128)(2,1)S(1)} %get-tuple-element.98), channel_id=1, source_target_pairs={{0,4},{1,5},{4,0},{5,1},{8,12},{9,13},{12,8},{13,9},{2,6},{3,7},{6... | collective-permute-start | bytes 1105928 | tf_op jit(solution)/shard_map/ppermute | solution.py:580
  (8 other events, 25.9 us)
